TPU v7x, 256 devices: a whole 4x4x8 slice. The times are simulated.
256 devices in a mesh: gx: 8 (over y, core), gy: 4 (over x), gz: 8 (over z).
Axes of the slice: x: 4, y: 4, z: 8, core: 2. Of those that a mesh axis runs over, the one named last changes fastest.
Arguments:
- magnetic: float32 [3, 128, 128, 1024], P(None, 'gx', 'gy', 'gz'), may hold values from -11 to 11
Outputs:
- cleaned: float32 [3, 128, 128, 1024], P(None, 'gx', 'gy', 'gz')
All inputs are finite; a program needn't handle non-finite values.
Results may differ from a plain program's by a relative error of at most 0.00018.
Values sent between devices are 32-bit elements; how exact they have to be, the bound alone decides.
A program may use at most 128 MiB of HBM per device.

v0:
```python
import jax
import jax.numpy as jnp
from jax import lax
from jax.sharding import PartitionSpec as P

LEVELS = 5
SWEEPS = 3
COARSE_ITERS = 24


relax_weight = 6.0 / 7.0


def extended(block, sides, width):
    for axis, dim in sides:
        count = lax.axis_size(axis)
        forward = [(i, i + 1) for i in range(count - 1)]
        forward.append((count - 1, 0))
        backward = [(target, source) for source, target in forward]
        low = lax.ppermute(
            lax.slice_in_dim(block, block.shape[dim] - width, None, axis=dim), axis, forward
        )
        high = lax.ppermute(lax.slice_in_dim(block, 0, width, axis=dim), axis, backward)
        block = jnp.concatenate([low, block, high], axis=dim)
    return block


def passed_along(value, axis, steps):
    count = lax.axis_size(axis)
    pairs = [(source, (source + steps) % count) for source in range(count)]
    return lax.ppermute(value, axis, pairs)


def faces(values, layers):
    return extended(values, (("gx", 0), ("gy", 1), ("gz", 2)), layers)


def apply_padded(padded, stretch):
    center = padded[1:-1, 1:-1, 1:-1]
    beside = padded[2:, 1:-1, 1:-1] + padded[:-2, 1:-1, 1:-1]
    beside = beside + padded[1:-1, 2:, 1:-1] + padded[1:-1, :-2, 1:-1]
    beside = beside + padded[1:-1, 1:-1, 2:] + padded[1:-1, 1:-1, :-2]
    return (6.0 * center - beside) * stretch


def apply_local(values, stretch):
    beside = jnp.roll(values, -1, 0) + jnp.roll(values, 1, 0)
    beside = beside + jnp.roll(values, -1, 1) + jnp.roll(values, 1, 1)
    beside = beside + jnp.roll(values, -1, 2) + jnp.roll(values, 1, 2)
    return (6.0 * values - beside) * stretch


def restrict(values):
    extent = values.shape
    blocks = values.reshape(extent[0] // 2, 2, extent[1] // 2, 2, extent[2] // 2, 2)
    return jnp.sum(blocks, axis=(1, 3, 5)) * 0.125


def prolong(values):
    extent = values.shape
    spread = jnp.broadcast_to(
        values[:, None, :, None, :, None], (extent[0], 2, extent[1], 2, extent[2], 2)
    )
    return spread.reshape(extent[0] * 2, extent[1] * 2, extent[2] * 2)


def cycle_whole(source, level_index):
    stretch = 0.25**level_index
    factor = relax_weight * 4.0**level_index / 6.0
    solution = factor * source

    def coarse_sweep(iteration, current):
        return current + factor * (source - apply_local(current, stretch))

    return lax.fori_loop(0, COARSE_ITERS - 1, coarse_sweep, solution)


def collect(source):
    extent = source.shape
    stacked = lax.all_gather(source[None], ("gx", "gy", "gz"), axis=0, tiled=True)
    count_x, count_y, count_z = (lax.axis_size("gx"), lax.axis_size("gy"), lax.axis_size("gz"))
    gathered_grid = stacked.reshape(count_x, count_y, count_z, extent[0], extent[1], extent[2])
    gathered_grid = gathered_grid.transpose(0, 3, 1, 4, 2, 5)
    return gathered_grid.reshape(count_x * extent[0], count_y * extent[1], count_z * extent[2])


def own_block(solution, extent):
    starts = (
        lax.axis_index("gx") * extent[0],
        lax.axis_index("gy") * extent[1],
        lax.axis_index("gz") * extent[2],
    )
    return lax.dynamic_slice(solution, starts, extent)


def cycle_shard(source, level_index, gather_level, deep_faces):
    extent = source.shape
    if level_index == gather_level:
        whole_grid = collect(source)
        return own_block(cycle_whole(whole_grid, level_index), extent)
    stretch = 0.25**level_index
    factor = relax_weight * 4.0**level_index / 6.0
    layers = SWEEPS
    solution = factor * source
    for repeat in range(layers - 1):
        padded = faces(solution, 1)
        solution = solution + factor * (source - apply_padded(padded, stretch))
    residual_field = source - apply_padded(faces(solution, 1), stretch)
    correction = cycle_shard(restrict(residual_field), level_index + 1, gather_level, deep_faces)
    solution = solution + prolong(correction)
    for repeat in range(layers):
        padded = faces(solution, 1)
        solution = solution + factor * (source - apply_padded(padded, stretch))
    return solution


def body(magnetic):
    along_x, along_y, along_z = (magnetic[0], magnetic[1], magnetic[2])
    below_x = passed_along(along_x[-1:], "gx", 1)
    below_y = passed_along(along_y[:, -1:], "gy", 1)
    below_z = passed_along(along_z[:, :, -1:], "gz", 1)
    lower_x = jnp.concatenate([below_x, along_x[:-1]], axis=0)
    lower_y = jnp.concatenate([below_y, along_y[:, :-1]], axis=1)
    lower_z = jnp.concatenate([below_z, along_z[:, :, :-1]], axis=2)
    divergence = along_x - lower_x + (along_y - lower_y) + (along_z - lower_z)
    gather_level = LEVELS - 1
    potential = cycle_shard(-divergence, 0, gather_level, False)
    padded = faces(potential, 1)
    center = padded[1:-1, 1:-1, 1:-1]
    cleaned_x = along_x - (padded[2:, 1:-1, 1:-1] - center)
    cleaned_y = along_y - (padded[1:-1, 2:, 1:-1] - center)
    cleaned_z = along_z - (padded[1:-1, 1:-1, 2:] - center)
    return jnp.stack([cleaned_x, cleaned_y, cleaned_z])


def solution(mesh):
    in_specs = (P(None, "gx", "gy", "gz"),)
    out_specs = P(None, "gx", "gy", "gz")
    return jax.shard_map(body, mesh=mesh, in_specs=in_specs, out_specs=out_specs, check_vma=False)
```

profile of v0, /device:TPU:1, one launch (start us, length us, event | category | flops | bytes accessed | tf_op | source)
XLA Modules:
  0.0 566.6 jit_solution(10184543052008542044)
XLA Ops:
  1.2 2.5 collective-permute-start.2
  5.8 2.4 collective-permute-start
  9.1 4.6 collective-permute-done.2
  18.9 2.6 collective-permute-start.5
  22.3 2.9 collective-permute-done.6
  27.0 4.9 collective-permute-done.7
  31.9 2.7 collective-permute-done.8
  34.9 6.0 %collective-permute-start.10 = (f32[1,32,128]{2,1,0:T(8,128)S(1)}, f32[1,32,128]{2,1,0:T(8,128)S(1)}, u32[]{:S(2)}, u32[]{:S(2)}) collective-permute-start(f32[1,32,128]{2,1,0:T(8,128)S(1)} %get-tuple-element.84), channel_id=1, source_target_pairs={{0,32},{32,64},{64,96},{96,128},{128,160},{160,192},{192,224},{224... | collective-permute-start | bytes 49160 | tf_op jit(solution)/shard_map/ppermute | solution.py:20
  41.8 2.3 collective-permute-done.9
  50.0 6.2 %collective-permute-done.13 = f32[18,34,1]{2,1,0:T(8,128)S(1)} collective-permute-done((f32[18,34,1]{2,1,0:T(8,128)S(1)}, f32[18,34,1]{2,1,0:T(8,128)S(1)}, u32[]{:S(2)}, u32[]{:S(2)}) %collective-permute-start.13) | collective-permute-done | bytes 2480 | tf_op jit(solution)/shard_map/ppermute | solution.py:23
  57.9 3.3 collective-permute-start.15
  69.3 1.7 collective-permute-start.20
  71.0 4.7 collective-permute-done.19
  77.5 18.1 %reshape.49 = f32[8,2,16,2,64,2]{5,4,3,2,1,0:T(8,128)} reshape(f32[16,32,128]{2,1,0:T(8,128)S(1)} %fusion.47) | data formatting | bytes 524288 | tf_op jit(solution)/shard_map/reshape | solution.py:55
  95.6 7.0 %reduce_sum.43 = f32[8,16,64]{2,1,0:T(8,128)S(1)} reduce(f32[8,2,16,2,64,2]{5,4,3,2,1,0:T(8,128)} %reshape.49, f32[]{:T(128)} %constant.15.clone.1), dimensions={1,3,5}, to_apply=%region_0.0 | reduce | flops 57344 | bytes 294916 | tf_op jit(solution)/shard_map/reduce_sum | solution.py:56
  102.6 6.0 %collective-permute-start.21 = (f32[1,16,64]{2,1,0:T(8,128)S(1)}, f32[1,16,64]{2,1,0:T(8,128)S(1)}, u32[]{:S(2)}, u32[]{:S(2)}) collective-permute-start(f32[1,16,64]{2,1,0:T(8,128)S(1)} %get-tuple-element.123), channel_id=1, source_target_pairs={{32,0},{64,32},{96,64},{128,96},{160,128},{192,160},{224,192},{0,2... | collective-permute-start | bytes 12296 | tf_op jit(solution)/shard_map/ppermute | solution.py:23
  116.1 2.6 collective-permute-done.25
  119.9 6.3 %collective-permute-start.27 = (f32[1,16,64]{2,1,0:T(8,128)S(1)}, f32[1,16,64]{2,1,0:T(8,128)S(1)}, u32[]{:S(2)}, u32[]{:S(2)}) collective-permute-start(f32[1,16,64]{2,1,0:T(8,128)S(1)} %get-tuple-element.121), channel_id=1, source_target_pairs={{32,0},{64,32},{96,64},{128,96},{160,128},{192,160},{224,192},{0,2... | collective-permute-start | bytes 12296 | tf_op jit(solution)/shard_map/ppermute | solution.py:23
  132.8 2.3 collective-permute-done.31
  136.6 5.6 collective-permute-start.33
  147.3 9.0 %collective-permute-start.37 = (f32[10,18,1]{2,1,0:T(8,128)S(1)}, f32[10,18,1]{2,1,0:T(8,128)S(1)}, u32[]{:S(2)}, u32[]{:S(2)}) collective-permute-start(f32[10,18,1]{2,1,0:T(8,128)S(1)} %get-tuple-element.94), channel_id=1, source_target_pairs={{1,0},{2,1},{3,2},{4,3},{5,4},{6,5},{7,6},{0,7},{9,8},{10,9},{11,1... | collective-permute-start | bytes 2168 | tf_op jit(solution)/shard_map/ppermute | solution.py:23
  157.7 2.3 collective-permute-done.37
  161.4 2.1 reshape.50
  163.8 5.6 collective-permute-start.39
  176.1 1.8 collective-permute-done.43
  179.1 5.7 %collective-permute-start.45 = (f32[1,8,32]{2,1,0:T(8,128)S(1)}, f32[1,8,32]{2,1,0:T(8,128)S(1)}, u32[]{:S(2)}, u32[]{:S(2)}) collective-permute-start(f32[1,8,32]{2,1,0:T(8,128)S(1)} %get-tuple-element.169), channel_id=1, source_target_pairs={{32,0},{64,32},{96,64},{128,96},{160,128},{192,160},{224,192},{0,2... | collective-permute-start | bytes 3080 | tf_op jit(solution)/shard_map/ppermute | solution.py:23
  194.5 5.7 %collective-permute-start.51 = (f32[1,8,32]{2,1,0:T(8,128)S(1)}, f32[1,8,32]{2,1,0:T(8,128)S(1)}, u32[]{:S(2)}, u32[]{:S(2)}) collective-permute-start(f32[1,8,32]{2,1,0:T(8,128)S(1)} %get-tuple-element.167), channel_id=1, source_target_pairs={{32,0},{64,32},{96,64},{128,96},{160,128},{192,160},{224,192},{0,2... | collective-permute-start | bytes 3080 | tf_op jit(solution)/shard_map/ppermute | solution.py:23
  210.0 5.6 collective-permute-start.57
  225.1 5.5 collective-permute-start.63
  240.0 5.7 %collective-permute-start.69 = (f32[1,4,16]{2,1,0:T(4,128)S(1)}, f32[1,4,16]{2,1,0:T(4,128)S(1)}, u32[]{:S(2)}, u32[]{:S(2)}) collective-permute-start(f32[1,4,16]{2,1,0:T(4,128)S(1)} %get-tuple-element.191), channel_id=1, source_target_pairs={{32,0},{64,32},{96,64},{128,96},{160,128},{192,160},{224,192},{0,2... | collective-permute-start | bytes 776 | tf_op jit(solution)/shard_map/ppermute | solution.py:23
  255.2 63.2 %all-gather.1 = f32[256,2,8]{2,1,0:T(2,128)S(1)} all-gather(f32[1,2,8]{2,1,0:T(2,128)S(1)} %multiply_bitcast_fusion), channel_id=2, replica_groups=mesh['gx'=8,'gy'=4,'gz'=8] {'gx','gy','gz'}, dimensions={0}, use_global_device_ids=true | all-gather | bytes 16448 | tf_op jit(solution)/shard_map/all_gather | solution.py:80
  318.6 7.3 %while.10 = (s32[]{:T(128)}, f32[8,8,64]{2,1,0:T(8,128)S(1)}, f32[8,8,64]{2,1,0:T(8,128)S(1)}, s32[]{:T(128)}) while((s32[]{:T(128)}, f32[8,8,64]{2,1,0:T(8,128)S(1)}, f32[8,8,64]{2,1,0:T(8,128)S(1)}, s32[]{:T(128)}) %tuple.114), condition=%wide.region_6.7_spmd, body=%wide.region_5.6_spmd.sunk | while | flops 69634 | bytes 344117 | solution.py:75
  326.1 3.6 collective-permute-start.75
  333.6 2.4 collective-permute-done.78
  336.1 2.2 collective-permute-start.79
  339.2 3.1 collective-permute-done.80
  342.4 6.0 %collective-permute-start.81 = (f32[1,4,16]{2,1,0:T(4,128)S(1)}, f32[1,4,16]{2,1,0:T(4,128)S(1)}, u32[]{:S(2)}, u32[]{:S(2)}) collective-permute-start(f32[1,4,16]{2,1,0:T(4,128)S(1)} %get-tuple-element.187), channel_id=1, source_target_pairs={{32,0},{64,32},{96,64},{128,96},{160,128},{192,160},{224,192},{0,2... | collective-permute-start | bytes 776 | tf_op jit(solution)/shard_map/ppermute | solution.py:23
  357.4 5.4 collective-permute-start.87
  372.2 5.4 collective-permute-start.93
  384.2 1.8 collective-permute-done.97
  387.0 4.2 collective-permute-start.100
  396.8 1.7 collective-permute-done.102
  402.0 1.7 collective-permute-done.104
  403.8 5.3 collective-permute-start.105
  418.9 1.6 reshape.55
  420.6 5.8 %collective-permute-start.111 = (f32[1,16,64]{2,1,0:T(8,128)S(1)}, f32[1,16,64]{2,1,0:T(8,128)S(1)}, u32[]{:S(2)}, u32[]{:S(2)}) collective-permute-start(f32[1,16,64]{2,1,0:T(8,128)S(1)} %get-tuple-element.117), channel_id=1, source_target_pairs={{32,0},{64,32},{96,64},{128,96},{160,128},{192,160},{224,192},{0,2... | collective-permute-start | bytes 12296 | tf_op jit(solution)/shard_map/ppermute | solution.py:23
  433.1 2.3 collective-permute-done.115
  436.9 5.5 collective-permute-start.117
  447.6 1.6 collective-permute-start.122
  449.2 2.1 collective-permute-done.121
  452.9 5.5 collective-permute-start.123
  465.3 2.5 collective-permute-done.127
  469.1 6.5 %broadcast_in_dim.37 = f32[8,2,16,2,64,2]{5,4,3,2,1,0:T(8,128)} broadcast(f32[8,16,64]{2,1,0:T(8,128)S(1)} %fusion.78), dimensions={0,2,4} | broadcast | bytes 294912 | tf_op jit(solution)/shard_map/broadcast_in_dim | solution.py:61
  475.6 12.7 %reshape.56 = f32[16,32,128]{2,1,0:T(8,128)S(1)} reshape(f32[8,2,16,2,64,2]{5,4,3,2,1,0:T(8,128)} %broadcast_in_dim.37) | data formatting | bytes 524288 | tf_op jit(solution)/shard_map/reshape | solution.py:64
  488.3 6.0 %collective-permute-start.129 = (f32[1,32,128]{2,1,0:T(8,128)S(1)}, f32[1,32,128]{2,1,0:T(8,128)S(1)}, u32[]{:S(2)}, u32[]{:S(2)}) collective-permute-start(f32[1,32,128]{2,1,0:T(8,128)S(1)} %get-tuple-element.81), channel_id=1, source_target_pairs={{32,0},{64,32},{96,64},{128,96},{160,128},{192,160},{224,192},{0,2... | collective-permute-start | bytes 49160 | tf_op jit(solution)/shard_map/ppermute | solution.py:23
  501.2 4.9 collective-permute-done.133
  507.8 5.9 %collective-permute-start.135 = (f32[1,32,128]{2,1,0:T(8,128)S(1)}, f32[1,32,128]{2,1,0:T(8,128)S(1)}, u32[]{:S(2)}, u32[]{:S(2)}) collective-permute-start(f32[1,32,128]{2,1,0:T(8,128)S(1)} %get-tuple-element.79), channel_id=1, source_target_pairs={{32,0},{64,32},{96,64},{128,96},{160,128},{192,160},{224,192},{0,2... | collective-permute-start | bytes 49160 | tf_op jit(solution)/shard_map/ppermute | solution.py:23
  519.1 1.6 collective-permute-start.140
  520.8 4.7 collective-permute-done.139
  527.4 5.5 collective-permute-start.141
  539.8 4.9 collective-permute-done.145
  546.3 5.9 %collective-permute-start.147 = (f32[1,32,128]{2,1,0:T(8,128)S(1)}, f32[1,32,128]{2,1,0:T(8,128)S(1)}, u32[]{:S(2)}, u32[]{:S(2)}) collective-permute-start(f32[1,32,128]{2,1,0:T(8,128)S(1)} %get-tuple-element.75), channel_id=1, source_target_pairs={{32,0},{64,32},{96,64},{128,96},{160,128},{192,160},{224,192},{0,2... | collective-permute-start | bytes 49160 | tf_op jit(solution)/shard_map/ppermute | solution.py:23
  553.1 1.7 collective-permute-done.148
  558.8 6.3 %collective-permute-done.151 = f32[18,34,1]{2,1,0:T(8,128)S(1)} collective-permute-done((f32[18,34,1]{2,1,0:T(8,128)S(1)}, f32[18,34,1]{2,1,0:T(8,128)S(1)}, u32[]{:S(2)}, u32[]{:S(2)}) %collective-permute-start.151) | collective-permute-done | bytes 2480 | tf_op jit(solution)/shard_map/ppermute | solution.py:23
  (565 shorter events, 221.2 us)
Async XLA Ops:
  1.2 12.5 %collective-permute-start.2 = (f32[16,32,1]{2,1,0:T(8,128)S(1)}, f32[16,32,1]{2,1,0:T(8,128)S(1)}, u32[]{:S(2)}, u32[]{:S(2)}) collective-permute-start(f32[16,32,1]{2,1,0:T(8,128)S(1)} %slice.1427), channel_id=1, source_target_pairs={{0,1},{1,2},{2,3},{3,4},{4,5},{5,6},{6,7},{7,0},{8,9},{9,10},{10,1... | collective-permute-start | bytes 6152 | tf_op jit(solution)/shard_map/ppermute | solution.py:31
  3.8 10.0 %collective-permute-start.1 = (f32[16,1,128]{2,1,0:T(1,128)S(1)}, f32[16,1,128]{2,1,0:T(1,128)S(1)}, u32[]{:S(2)}, u32[]{:S(2)}) collective-permute-start(f32[16,1,128]{2,1,0:T(1,128)S(1)} %slice.1425), channel_id=1, source_target_pairs={{0,8},{8,16},{16,24},{24,0},{1,9},{9,17},{17,25},{25,1},{2,10},{10... | collective-permute-start | bytes 24584 | tf_op jit(solution)/shard_map/ppermute | solution.py:31
  5.8 8.0 %collective-permute-start = (f32[1,32,128]{2,1,0:T(8,128)S(1)}, f32[1,32,128]{2,1,0:T(8,128)S(1)}, u32[]{:S(2)}, u32[]{:S(2)}) collective-permute-start(f32[1,32,128]{2,1,0:T(8,128)S(1)} %slice_bitcast_fusion.3), channel_id=1, source_target_pairs={{0,32},{32,64},{64,96},{96,128},{128,160},{160,192},{192,224},{224... | collective-permute-start | bytes 49160 | tf_op jit(solution)/shard_map/ppermute | solution.py:31
  15.0 3.8 collective-permute-start.3
  25.4 6.4 %collective-permute-start.7 = (f32[18,34,1]{2,1,0:T(8,128)S(1)}, f32[18,34,1]{2,1,0:T(8,128)S(1)}, u32[]{:S(2)}, u32[]{:S(2)}) collective-permute-start(f32[18,34,1]{2,1,0:T(8,128)S(1)} %get-tuple-element.58), channel_id=1, source_target_pairs={{1,0},{2,1},{3,2},{4,3},{5,4},{6,5},{7,6},{0,7},{9,8},{10,9},{11,1... | collective-permute-start | bytes 7352 | tf_op jit(solution)/shard_map/ppermute | solution.py:23
  27.0 7.6 %collective-permute-start.8 = (f32[18,34,1]{2,1,0:T(8,128)S(1)}, f32[18,34,1]{2,1,0:T(8,128)S(1)}, u32[]{:S(2)}, u32[]{:S(2)}) collective-permute-start(f32[18,34,1]{2,1,0:T(8,128)S(1)} %get-tuple-element.59), channel_id=1, source_target_pairs={{0,1},{1,2},{2,3},{3,4},{4,5},{5,6},{6,7},{7,0},{8,9},{9,10},{10,1... | collective-permute-start | bytes 7352 | tf_op jit(solution)/shard_map/ppermute | solution.py:20
  34.9 6.9 %collective-permute-start.10 = (f32[1,32,128]{2,1,0:T(8,128)S(1)}, f32[1,32,128]{2,1,0:T(8,128)S(1)}, u32[]{:S(2)}, u32[]{:S(2)}) collective-permute-start(f32[1,32,128]{2,1,0:T(8,128)S(1)} %get-tuple-element.84), channel_id=1, source_target_pairs={{0,32},{32,64},{64,96},{96,128},{128,160},{160,192},{192,224},{224... | collective-permute-start | bytes 49160 | tf_op jit(solution)/shard_map/ppermute | solution.py:20
  48.5 7.8 %collective-permute-start.13 = (f32[18,34,1]{2,1,0:T(8,128)S(1)}, f32[18,34,1]{2,1,0:T(8,128)S(1)}, u32[]{:S(2)}, u32[]{:S(2)}) collective-permute-start(f32[18,34,1]{2,1,0:T(8,128)S(1)} %get-tuple-element.56), channel_id=1, source_target_pairs={{1,0},{2,1},{3,2},{4,3},{5,4},{6,5},{7,6},{0,7},{9,8},{10,9},{11,1... | collective-permute-start | bytes 7352 | tf_op jit(solution)/shard_map/ppermute | solution.py:23
  48.6 8.9 %collective-permute-start.14 = (f32[18,34,1]{2,1,0:T(8,128)S(1)}, f32[18,34,1]{2,1,0:T(8,128)S(1)}, u32[]{:S(2)}, u32[]{:S(2)}) collective-permute-start(f32[18,34,1]{2,1,0:T(8,128)S(1)} %get-tuple-element.57), channel_id=1, source_target_pairs={{0,1},{1,2},{2,3},{3,4},{4,5},{5,6},{6,7},{7,0},{8,9},{9,10},{10,1... | collective-permute-start | bytes 7352 | tf_op jit(solution)/shard_map/ppermute | solution.py:20
  57.9 5.6 collective-permute-start.15
  69.2 6.4 %collective-permute-start.19 = (f32[18,34,1]{2,1,0:T(8,128)S(1)}, f32[18,34,1]{2,1,0:T(8,128)S(1)}, u32[]{:S(2)}, u32[]{:S(2)}) collective-permute-start(f32[18,34,1]{2,1,0:T(8,128)S(1)} %get-tuple-element.54), channel_id=1, source_target_pairs={{1,0},{2,1},{3,2},{4,3},{5,4},{6,5},{7,6},{0,7},{9,8},{10,9},{11,1... | collective-permute-start | bytes 7352 | tf_op jit(solution)/shard_map/ppermute | solution.py:23
  69.3 7.9 %collective-permute-start.20 = (f32[18,34,1]{2,1,0:T(8,128)S(1)}, f32[18,34,1]{2,1,0:T(8,128)S(1)}, u32[]{:S(2)}, u32[]{:S(2)}) collective-permute-start(f32[18,34,1]{2,1,0:T(8,128)S(1)} %get-tuple-element.55), channel_id=1, source_target_pairs={{0,1},{1,2},{2,3},{3,4},{4,5},{5,6},{6,7},{7,0},{8,9},{9,10},{10,1... | collective-permute-start | bytes 7352 | tf_op jit(solution)/shard_map/ppermute | solution.py:20
  102.6 6.8 %collective-permute-start.21 = (f32[1,16,64]{2,1,0:T(8,128)S(1)}, f32[1,16,64]{2,1,0:T(8,128)S(1)}, u32[]{:S(2)}, u32[]{:S(2)}) collective-permute-start(f32[1,16,64]{2,1,0:T(8,128)S(1)} %get-tuple-element.123), channel_id=1, source_target_pairs={{32,0},{64,32},{96,64},{128,96},{160,128},{192,160},{224,192},{0,2... | collective-permute-start | bytes 12296 | tf_op jit(solution)/shard_map/ppermute | solution.py:23
  114.6 4.1 collective-permute-start.25
  114.7 5.0 collective-permute-start.26
  119.9 7.1 %collective-permute-start.27 = (f32[1,16,64]{2,1,0:T(8,128)S(1)}, f32[1,16,64]{2,1,0:T(8,128)S(1)}, u32[]{:S(2)}, u32[]{:S(2)}) collective-permute-start(f32[1,16,64]{2,1,0:T(8,128)S(1)} %get-tuple-element.121), channel_id=1, source_target_pairs={{32,0},{64,32},{96,64},{128,96},{160,128},{192,160},{224,192},{0,2... | collective-permute-start | bytes 12296 | tf_op jit(solution)/shard_map/ppermute | solution.py:23
  131.3 3.9 collective-permute-start.31
  131.4 5.0 collective-permute-start.32
  136.6 6.4 %collective-permute-start.33 = (f32[1,16,64]{2,1,0:T(8,128)S(1)}, f32[1,16,64]{2,1,0:T(8,128)S(1)}, u32[]{:S(2)}, u32[]{:S(2)}) collective-permute-start(f32[1,16,64]{2,1,0:T(8,128)S(1)} %get-tuple-element.119), channel_id=1, source_target_pairs={{32,0},{64,32},{96,64},{128,96},{160,128},{192,160},{224,192},{0,2... | collective-permute-start | bytes 12296 | tf_op jit(solution)/shard_map/ppermute | solution.py:23
  147.3 12.7 %collective-permute-start.37 = (f32[10,18,1]{2,1,0:T(8,128)S(1)}, f32[10,18,1]{2,1,0:T(8,128)S(1)}, u32[]{:S(2)}, u32[]{:S(2)}) collective-permute-start(f32[10,18,1]{2,1,0:T(8,128)S(1)} %get-tuple-element.94), channel_id=1, source_target_pairs={{1,0},{2,1},{3,2},{4,3},{5,4},{6,5},{7,6},{0,7},{9,8},{10,9},{11,1... | collective-permute-start | bytes 2168 | tf_op jit(solution)/shard_map/ppermute | solution.py:23
  156.3 5.0 collective-permute-start.38
  163.8 6.5 %collective-permute-start.39 = (f32[1,8,32]{2,1,0:T(8,128)S(1)}, f32[1,8,32]{2,1,0:T(8,128)S(1)}, u32[]{:S(2)}, u32[]{:S(2)}) collective-permute-start(f32[1,8,32]{2,1,0:T(8,128)S(1)} %get-tuple-element.171), channel_id=1, source_target_pairs={{32,0},{64,32},{96,64},{128,96},{160,128},{192,160},{224,192},{0,2... | collective-permute-start | bytes 3080 | tf_op jit(solution)/shard_map/ppermute | solution.py:23
  174.9 4.2 collective-permute-start.44
  179.1 6.6 %collective-permute-start.45 = (f32[1,8,32]{2,1,0:T(8,128)S(1)}, f32[1,8,32]{2,1,0:T(8,128)S(1)}, u32[]{:S(2)}, u32[]{:S(2)}) collective-permute-start(f32[1,8,32]{2,1,0:T(8,128)S(1)} %get-tuple-element.169), channel_id=1, source_target_pairs={{32,0},{64,32},{96,64},{128,96},{160,128},{192,160},{224,192},{0,2... | collective-permute-start | bytes 3080 | tf_op jit(solution)/shard_map/ppermute | solution.py:23
  190.2 4.2 collective-permute-start.50
  194.5 6.5 %collective-permute-start.51 = (f32[1,8,32]{2,1,0:T(8,128)S(1)}, f32[1,8,32]{2,1,0:T(8,128)S(1)}, u32[]{:S(2)}, u32[]{:S(2)}) collective-permute-start(f32[1,8,32]{2,1,0:T(8,128)S(1)} %get-tuple-element.167), channel_id=1, source_target_pairs={{32,0},{64,32},{96,64},{128,96},{160,128},{192,160},{224,192},{0,2... | collective-permute-start | bytes 3080 | tf_op jit(solution)/shard_map/ppermute | solution.py:23
  205.4 4.2 collective-permute-start.56
  210.0 6.4 %collective-permute-start.57 = (f32[1,4,16]{2,1,0:T(4,128)S(1)}, f32[1,4,16]{2,1,0:T(4,128)S(1)}, u32[]{:S(2)}, u32[]{:S(2)}) collective-permute-start(f32[1,4,16]{2,1,0:T(4,128)S(1)} %get-tuple-element.195), channel_id=1, source_target_pairs={{32,0},{64,32},{96,64},{128,96},{160,128},{192,160},{224,192},{0,2... | collective-permute-start | bytes 776 | tf_op jit(solution)/shard_map/ppermute | solution.py:23
  221.1 3.9 collective-permute-start.62
  225.1 6.3 %collective-permute-start.63 = (f32[1,4,16]{2,1,0:T(4,128)S(1)}, f32[1,4,16]{2,1,0:T(4,128)S(1)}, u32[]{:S(2)}, u32[]{:S(2)}) collective-permute-start(f32[1,4,16]{2,1,0:T(4,128)S(1)} %get-tuple-element.193), channel_id=1, source_target_pairs={{32,0},{64,32},{96,64},{128,96},{160,128},{192,160},{224,192},{0,2... | collective-permute-start | bytes 776 | tf_op jit(solution)/shard_map/ppermute | solution.py:23
  240.0 6.5 %collective-permute-start.69 = (f32[1,4,16]{2,1,0:T(4,128)S(1)}, f32[1,4,16]{2,1,0:T(4,128)S(1)}, u32[]{:S(2)}, u32[]{:S(2)}) collective-permute-start(f32[1,4,16]{2,1,0:T(4,128)S(1)} %get-tuple-element.191), channel_id=1, source_target_pairs={{32,0},{64,32},{96,64},{128,96},{160,128},{192,160},{224,192},{0,2... | collective-permute-start | bytes 776 | tf_op jit(solution)/shard_map/ppermute | solution.py:23
  250.9 4.0 collective-permute-start.74
  326.1 4.5 collective-permute-start.75
  338.3 4.0 collective-permute-start.80
  342.4 6.8 %collective-permute-start.81 = (f32[1,4,16]{2,1,0:T(4,128)S(1)}, f32[1,4,16]{2,1,0:T(4,128)S(1)}, u32[]{:S(2)}, u32[]{:S(2)}) collective-permute-start(f32[1,4,16]{2,1,0:T(4,128)S(1)} %get-tuple-element.187), channel_id=1, source_target_pairs={{32,0},{64,32},{96,64},{128,96},{160,128},{192,160},{224,192},{0,2... | collective-permute-start | bytes 776 | tf_op jit(solution)/shard_map/ppermute | solution.py:23
  353.4 3.9 collective-permute-start.86
  357.4 6.2 %collective-permute-start.87 = (f32[1,4,16]{2,1,0:T(4,128)S(1)}, f32[1,4,16]{2,1,0:T(4,128)S(1)}, u32[]{:S(2)}, u32[]{:S(2)}) collective-permute-start(f32[1,4,16]{2,1,0:T(4,128)S(1)} %get-tuple-element.185), channel_id=1, source_target_pairs={{32,0},{64,32},{96,64},{128,96},{160,128},{192,160},{224,192},{0,2... | collective-permute-start | bytes 776 | tf_op jit(solution)/shard_map/ppermute | solution.py:23
  367.9 3.9 collective-permute-start.92
  372.2 6.2 %collective-permute-start.93 = (f32[1,8,32]{2,1,0:T(8,128)S(1)}, f32[1,8,32]{2,1,0:T(8,128)S(1)}, u32[]{:S(2)}, u32[]{:S(2)}) collective-permute-start(f32[1,8,32]{2,1,0:T(8,128)S(1)} %get-tuple-element.153), channel_id=1, source_target_pairs={{32,0},{64,32},{96,64},{128,96},{160,128},{192,160},{224,192},{0,2... | collective-permute-start | bytes 3080 | tf_op jit(solution)/shard_map/ppermute | solution.py:23
  382.7 4.2 collective-permute-start.98
  387.0 6.1 %collective-permute-start.100 = (f32[1,8,32]{2,1,0:T(8,128)S(1)}, f32[1,8,32]{2,1,0:T(8,128)S(1)}, u32[]{:S(2)}, u32[]{:S(2)}) collective-permute-start(f32[1,8,32]{2,1,0:T(8,128)S(1)} %get-tuple-element.150), channel_id=1, source_target_pairs={{0,32},{32,64},{64,96},{96,128},{128,160},{160,192},{192,224},{224... | collective-permute-start | bytes 3080 | tf_op jit(solution)/shard_map/ppermute | solution.py:20
  399.5 4.2 collective-permute-start.104
  403.8 6.2 %collective-permute-start.105 = (f32[1,8,32]{2,1,0:T(8,128)S(1)}, f32[1,8,32]{2,1,0:T(8,128)S(1)}, u32[]{:S(2)}, u32[]{:S(2)}) collective-permute-start(f32[1,8,32]{2,1,0:T(8,128)S(1)} %get-tuple-element.149), channel_id=1, source_target_pairs={{32,0},{64,32},{96,64},{128,96},{160,128},{192,160},{224,192},{0,2... | collective-permute-start | bytes 3080 | tf_op jit(solution)/shard_map/ppermute | solution.py:23
  414.3 4.2 collective-permute-start.110
  420.6 6.7 %collective-permute-start.111 = (f32[1,16,64]{2,1,0:T(8,128)S(1)}, f32[1,16,64]{2,1,0:T(8,128)S(1)}, u32[]{:S(2)}, u32[]{:S(2)}) collective-permute-start(f32[1,16,64]{2,1,0:T(8,128)S(1)} %get-tuple-element.117), channel_id=1, source_target_pairs={{32,0},{64,32},{96,64},{128,96},{160,128},{192,160},{224,192},{0,2... | collective-permute-start | bytes 12296 | tf_op jit(solution)/shard_map/ppermute | solution.py:23
  431.6 3.8 collective-permute-start.115
  431.7 5.0 collective-permute-start.116
  436.9 6.3 %collective-permute-start.117 = (f32[1,16,64]{2,1,0:T(8,128)S(1)}, f32[1,16,64]{2,1,0:T(8,128)S(1)}, u32[]{:S(2)}, u32[]{:S(2)}) collective-permute-start(f32[1,16,64]{2,1,0:T(8,128)S(1)} %get-tuple-element.115), channel_id=1, source_target_pairs={{32,0},{64,32},{96,64},{128,96},{160,128},{192,160},{224,192},{0,2... | collective-permute-start | bytes 12296 | tf_op jit(solution)/shard_map/ppermute | solution.py:23
  447.5 3.8 collective-permute-start.121
  447.6 5.2 collective-permute-start.122
  452.9 6.3 %collective-permute-start.123 = (f32[1,16,64]{2,1,0:T(8,128)S(1)}, f32[1,16,64]{2,1,0:T(8,128)S(1)}, u32[]{:S(2)}, u32[]{:S(2)}) collective-permute-start(f32[1,16,64]{2,1,0:T(8,128)S(1)} %get-tuple-element.113), channel_id=1, source_target_pairs={{32,0},{64,32},{96,64},{128,96},{160,128},{192,160},{224,192},{0,2... | collective-permute-start | bytes 12296 | tf_op jit(solution)/shard_map/ppermute | solution.py:23
  463.7 4.0 collective-permute-start.127
  464.0 4.9 collective-permute-start.128
  488.3 6.8 %collective-permute-start.129 = (f32[1,32,128]{2,1,0:T(8,128)S(1)}, f32[1,32,128]{2,1,0:T(8,128)S(1)}, u32[]{:S(2)}, u32[]{:S(2)}) collective-permute-start(f32[1,32,128]{2,1,0:T(8,128)S(1)} %get-tuple-element.81), channel_id=1, source_target_pairs={{32,0},{64,32},{96,64},{128,96},{160,128},{192,160},{224,192},{0,2... | collective-permute-start | bytes 49160 | tf_op jit(solution)/shard_map/ppermute | solution.py:23
  499.7 6.4 %collective-permute-start.133 = (f32[18,34,1]{2,1,0:T(8,128)S(1)}, f32[18,34,1]{2,1,0:T(8,128)S(1)}, u32[]{:S(2)}, u32[]{:S(2)}) collective-permute-start(f32[18,34,1]{2,1,0:T(8,128)S(1)} %get-tuple-element.52), channel_id=1, source_target_pairs={{1,0},{2,1},{3,2},{4,3},{5,4},{6,5},{7,6},{0,7},{9,8},{10,9},{11,1... | collective-permute-start | bytes 7352 | tf_op jit(solution)/shard_map/ppermute | solution.py:23
  499.8 7.7 %collective-permute-start.134 = (f32[18,34,1]{2,1,0:T(8,128)S(1)}, f32[18,34,1]{2,1,0:T(8,128)S(1)}, u32[]{:S(2)}, u32[]{:S(2)}) collective-permute-start(f32[18,34,1]{2,1,0:T(8,128)S(1)} %get-tuple-element.53), channel_id=1, source_target_pairs={{0,1},{1,2},{2,3},{3,4},{4,5},{5,6},{6,7},{7,0},{8,9},{9,10},{10,1... | collective-permute-start | bytes 7352 | tf_op jit(solution)/shard_map/ppermute | solution.py:20
  507.8 6.8 %collective-permute-start.135 = (f32[1,32,128]{2,1,0:T(8,128)S(1)}, f32[1,32,128]{2,1,0:T(8,128)S(1)}, u32[]{:S(2)}, u32[]{:S(2)}) collective-permute-start(f32[1,32,128]{2,1,0:T(8,128)S(1)} %get-tuple-element.79), channel_id=1, source_target_pairs={{32,0},{64,32},{96,64},{128,96},{160,128},{192,160},{224,192},{0,2... | collective-permute-start | bytes 49160 | tf_op jit(solution)/shard_map/ppermute | solution.py:23
  519.0 6.4 %collective-permute-start.139 = (f32[18,34,1]{2,1,0:T(8,128)S(1)}, f32[18,34,1]{2,1,0:T(8,128)S(1)}, u32[]{:S(2)}, u32[]{:S(2)}) collective-permute-start(f32[18,34,1]{2,1,0:T(8,128)S(1)} %get-tuple-element.50), channel_id=1, source_target_pairs={{1,0},{2,1},{3,2},{4,3},{5,4},{6,5},{7,6},{0,7},{9,8},{10,9},{11,1... | collective-permute-start | bytes 7352 | tf_op jit(solution)/shard_map/ppermute | solution.py:23
  519.1 7.9 %collective-permute-start.140 = (f32[18,34,1]{2,1,0:T(8,128)S(1)}, f32[18,34,1]{2,1,0:T(8,128)S(1)}, u32[]{:S(2)}, u32[]{:S(2)}) collective-permute-start(f32[18,34,1]{2,1,0:T(8,128)S(1)} %get-tuple-element.51), channel_id=1, source_target_pairs={{0,1},{1,2},{2,3},{3,4},{4,5},{5,6},{6,7},{7,0},{8,9},{9,10},{10,1... | collective-permute-start | bytes 7352 | tf_op jit(solution)/shard_map/ppermute | solution.py:20
  527.4 6.4 %collective-permute-start.141 = (f32[1,32,128]{2,1,0:T(8,128)S(1)}, f32[1,32,128]{2,1,0:T(8,128)S(1)}, u32[]{:S(2)}, u32[]{:S(2)}) collective-permute-start(f32[1,32,128]{2,1,0:T(8,128)S(1)} %get-tuple-element.77), channel_id=1, source_target_pairs={{32,0},{64,32},{96,64},{128,96},{160,128},{192,160},{224,192},{0,2... | collective-permute-start | bytes 49160 | tf_op jit(solution)/shard_map/ppermute | solution.py:23
  538.2 6.4 %collective-permute-start.145 = (f32[18,34,1]{2,1,0:T(8,128)S(1)}, f32[18,34,1]{2,1,0:T(8,128)S(1)}, u32[]{:S(2)}, u32[]{:S(2)}) collective-permute-start(f32[18,34,1]{2,1,0:T(8,128)S(1)} %get-tuple-element.48), channel_id=1, source_target_pairs={{1,0},{2,1},{3,2},{4,3},{5,4},{6,5},{7,6},{0,7},{9,8},{10,9},{11,1... | collective-permute-start | bytes 7352 | tf_op jit(solution)/shard_map/ppermute | solution.py:23
  538.3 7.7 %collective-permute-start.146 = (f32[18,34,1]{2,1,0:T(8,128)S(1)}, f32[18,34,1]{2,1,0:T(8,128)S(1)}, u32[]{:S(2)}, u32[]{:S(2)}) collective-permute-start(f32[18,34,1]{2,1,0:T(8,128)S(1)} %get-tuple-element.49), channel_id=1, source_target_pairs={{0,1},{1,2},{2,3},{3,4},{4,5},{5,6},{6,7},{7,0},{8,9},{9,10},{10,1... | collective-permute-start | bytes 7352 | tf_op jit(solution)/shard_map/ppermute | solution.py:20
  546.3 6.8 %collective-permute-start.147 = (f32[1,32,128]{2,1,0:T(8,128)S(1)}, f32[1,32,128]{2,1,0:T(8,128)S(1)}, u32[]{:S(2)}, u32[]{:S(2)}) collective-permute-start(f32[1,32,128]{2,1,0:T(8,128)S(1)} %get-tuple-element.75), channel_id=1, source_target_pairs={{32,0},{64,32},{96,64},{128,96},{160,128},{192,160},{224,192},{0,2... | collective-permute-start | bytes 49160 | tf_op jit(solution)/shard_map/ppermute | solution.py:23
  558.7 6.4 %collective-permute-start.151 = (f32[18,34,1]{2,1,0:T(8,128)S(1)}, f32[18,34,1]{2,1,0:T(8,128)S(1)}, u32[]{:S(2)}, u32[]{:S(2)}) collective-permute-start(f32[18,34,1]{2,1,0:T(8,128)S(1)} %pad_maximum_fusion.1), channel_id=1, source_target_pairs={{1,0},{2,1},{3,2},{4,3},{5,4},{6,5},{7,6},{0,7},{9,8},{10,9},{11,1... | collective-permute-start | bytes 7352 | tf_op jit(solution)/shard_map/ppermute | solution.py:23
  (89 other events, 329.8 us)
where the time goes:
time: 575 us; the launch traced here: 567 us
  starting transfers between devices  229 us (40%)
  waiting for transfers between devices  203 us (35%)
  blocking collectives  63.2 us (11%)
  local copies, waits for them, and re-layouts  51.6 us (9%)
  other arithmetic  17.5 us (3%)
    ppermute x75, starting transfers between devices, extended(): lax.ppermute(lax.slice_in_dim(block, 0, width, axis=dim), axis, backward)  147 us
    ppermute x75, waiting for transfers between devices, extended(): lax.ppermute(lax.slice_in_dim(block, 0, width, axis=dim), axis, backward)  119 us
    ppermute x74, waiting for transfers between devices, extended(): lax.ppermute(lax.slice_in_dim(block, block.shape[dim] - width, None, axis...  79.3 us
    ppermute x74, starting transfers between devices, extended(): lax.ppermute(lax.slice_in_dim(block, block.shape[dim] - width, None, axis...  75.5 us
    all_gather x1, blocking collectives, collect(): lax.all_gather(source[None], ('gx', 'gy', 'gz'), axis=0, tiled=True)  63.2 us
    reshape x3, local copies, waits for them, and re-layouts, restrict(): values.reshape(extent[0] // 2, 2, extent[1] // 2, 2, extent[2] // 2, 2)  20.4 us
    reshape x3, local copies, waits for them, and re-layouts, prolong(): return spread.reshape(extent[0] * 2, extent[1] * 2, extent[2] * 2)  14.5 us
  transfers between devices with their start and end apart: 152, of which 149 were waited for; matrix products, arithmetic and copies ran while one was open for 0% of the time, Pallas kernels for 0%

commit v1 on v0

v1 whole, which is shorter than its diff:
```python
import functools
import itertools

import jax
import jax.numpy as jnp
from jax import lax
from jax.experimental import pallas as pl
from jax.experimental.pallas import tpu as pltpu
from jax.sharding import PartitionSpec as P

SWEEPS = 3
COARSE_ITERS = 24
MESH = pl.DeviceIdType.MESH
F32 = jnp.float32
NEAR = [d for d in itertools.product((-1, 0, 1), repeat=3) if d != (0, 0, 0)]
WIDE = NEAR + [(dx, dy, dz) for dx in (-2, 2) for dy in (-1, 0, 1) for dz in (-1, 0, 1)]
COUNT_X, COUNT_Y, COUNT_Z = 8, 4, 8
PLANE = [(a, b) for a in range(COUNT_X) for b in range(COUNT_Y) if (a, b) != (0, 0)]
SEVENTH = 1.0 / 7.0


def lane_of(shape):
    return lax.broadcasted_iota(jnp.int32, shape, len(shape) - 1)


def row_of(shape):
    return lax.broadcasted_iota(jnp.int32, shape, len(shape) - 2)


def turned(value, shift, axis):
    shift = shift % value.shape[axis]
    return value if shift == 0 else pltpu.roll(value, shift, axis)


def mixed(center, low, high):
    rows, lanes = center.ndim - 2, center.ndim - 1
    total = center + low + high
    total = total + (turned(center, 1, rows) + turned(center, -1, rows))
    total = total + (turned(center, 1, lanes) + turned(center, -1, lanes))
    return total * SEVENTH


def sweep(target, current, source, low, high, step):
    def body(index, carry):
        at = low + index * step
        mean = mixed(
            current[pl.ds(at, step)], current[pl.ds(at - 1, step)], current[pl.ds(at + 1, step)]
        )
        target[pl.ds(at, step)] = mean + source[pl.ds(at, step)]
        return carry

    lax.fori_loop(0, (high - low) // step, body, 0)


def residual_pair(current, source, at):
    center = current[pl.ds(at, 2)]
    mean = mixed(center, current[pl.ds(at - 1, 2)], current[pl.ds(at + 1, 2)])
    value = mean + source[pl.ds(at, 2)] - center
    return value[0] + value[1]


def selected(value, matrix):
    high = value.astype(jnp.bfloat16)
    low = (value - high.astype(F32)).astype(jnp.bfloat16)
    return jnp.dot(high, matrix, preferred_element_type=F32) + jnp.dot(
        low, matrix, preferred_element_type=F32
    )


def halving(period):
    lane, row = lane_of((128, 128)), row_of((128, 128))
    return jnp.where(row // 2 == lane % period, 0.5, 0.0).astype(jnp.bfloat16)


def doubling(lanes, wrap):
    lane, row = lane_of((128, lanes)), row_of((128, lanes))
    origin = lane // 2
    if wrap:
        origin = origin + jnp.where(lane >= 96, 64, 0)
    return jnp.where(row == origin, 1.0, 0.0).astype(jnp.bfloat16)


def row_pairs(ref, count, rows):
    pieces = [
        ref[index, pl.ds(0, rows, stride=2), :] + ref[index, pl.ds(1, rows, stride=2), :]
        for index in range(count)
    ]
    return jnp.concatenate(pieces, axis=0)


def kernel(magnetic, cleaned, *scratch):
    (
        field, result, low_x, low_y, low_z, last_y, last_z,
        source0, first0, second0, packed0, sides0, pairs0, spread0,
        slabs1, packed1, sides1, source1, first1, second1, pairs1, spread1,
        packed2, blocks2, source2, first2, second2, pairs2, spread2,
        lines3, gathered3, source3, level3, pairs3,
        load_sem, store_sem,
        send_a, recv_a, send_b, recv_b, send_c, recv_c, send_d, recv_d, send_e, recv_e, send_f, recv_f,
    ) = scratch
    me = (lax.axis_index("gx"), lax.axis_index("gy"), lax.axis_index("gz"))
    counts = (COUNT_X, COUNT_Y, COUNT_Z)

    def at(offset):
        return tuple(lax.rem(m + o + c, c) for m, o, c in zip(me, offset, counts))

    def remote(source, target, sends, recvs, index, offset):
        return pltpu.make_async_remote_copy(
            src_ref=source, dst_ref=target, send_sem=sends.at[index], recv_sem=recvs.at[index],
            device_id=at(offset), device_id_type=MESH,
        )

    pending = []

    def launch(copies):
        for copy in copies:
            copy.start()
        pending.extend(copies)

    def arrive(copies):
        for copy in copies:
            copy.wait_recv()

    loads = [pltpu.make_async_copy(magnetic.at[c], field.at[c], load_sem.at[c]) for c in range(3)]
    for load in loads:
        load.start()
    barrier = pltpu.get_barrier_semaphore()
    for offset in NEAR:
        pl.semaphore_signal(barrier, inc=1, device_id=at(offset), device_id_type=MESH)
    for load in loads:
        load.wait()

    lane32 = lane_of((32, 128))
    row32 = row_of((32, 128))

    last_y[...] = field[1, pl.ds(31, 16, stride=32), :]
    column = jnp.zeros((32, 128), F32)
    for x in range(16):
        column = jnp.where(
            lane32 == x, turned(field[2, x * 32 : x * 32 + 32, :], x + 1, 1), column
        )
    last_z[...] = column
    pl.semaphore_wait(barrier, len(NEAR))
    round_a = [
        remote(field.at[0, pl.ds(480, 32)], low_x, send_a, recv_a, 0, (1, 0, 0)),
        remote(last_y, low_y, send_a, recv_a, 1, (0, 1, 0)),
        remote(last_z, low_z, send_a, recv_a, 2, (0, 0, 1)),
    ]
    launch(round_a)
    arrive(round_a)

    column = low_z[...]
    halves = []
    edge = (lane32 < 8) | (lane32 >= 120)
    for half in range(2):
        total = jnp.zeros((32, 128), F32)
        for slot in range(8):
            x = half * 8 + slot
            own_x = field[0, x * 32 : x * 32 + 32, :]
            below_x = low_x[...] if x == 0 else field[0, x * 32 - 32 : x * 32, :]
            own_y = field[1, x * 32 : x * 32 + 32, :]
            below_y = jnp.where(row32 == 0, low_y[x : x + 1, :], turned(own_y, 1, 0))
            own_z = field[2, x * 32 : x * 32 + 32, :]
            below_z = jnp.where(lane32 == 0, turned(column, -x, 1), turned(own_z, 1, 1))
            value = ((below_x - own_x) + (below_y - own_y) + (below_z - own_z)) * SEVENTH
            source0[6 + x, 8:40, 0:128] = value
            total = total + turned(jnp.where(edge, value, 0.0), slot * 16, 1)
        packed0[:, half * 128 : half * 128 + 128] = total

    rows_from = {-1: (24, 8), 0: (0, 32), 1: (0, 8)}
    rows_to = {-1: 0, 0: 8, 1: 40}
    planes_from = {-1: (10, 6), 0: (0, 16), 1: (0, 6)}
    planes_to = {-1: 0, 0: 6, 1: 22}
    lanes_from = {-1: (128, 128), 0: (0, 256), 1: (0, 128)}
    lanes_to = {-1: 0, 0: 128, 1: 384}
    round_b = []
    for index, (dx, dy, dz) in enumerate(NEAR):
        (row, rows), peer = rows_from[dy], (-dx, -dy, -dz)
        if dz == 0:
            plane, planes = planes_from[dx]
            origin = source0.at[pl.ds(6 + plane, planes), pl.ds(8 + row, rows), pl.ds(0, 128)]
            target = source0.at[pl.ds(planes_to[dx], planes), pl.ds(rows_to[dy], rows), pl.ds(0, 128)]
        else:
            lane, lanes = lanes_from[dx]
            origin = packed0.at[pl.ds(row, rows), pl.ds(lane, lanes)]
            target = sides0.at[(dz + 1) // 2, pl.ds(rows_to[dy], rows), pl.ds(lanes_to[dx], lanes)]
        round_b.append(remote(origin, target, send_b, recv_b, index, peer))
    launch(round_b)
    arrive(round_b)

    lane48 = lane_of((48, 128))
    for group in range(4):
        lanes = slice(group * 128, group * 128 + 128)
        joined = jnp.where((lane48 // 8) % 2 == 1, sides0[0, :, lanes], sides0[1, :, lanes])
        for slot in range(8):
            x = group * 8 + slot - 8
            if -6 <= x < 22:
                source0[6 + x, :, 128:256] = turned(joined, -16 * slot, 1)
    sweep(first0, source0, source0, 1, 27, 2)
    sweep(second0, first0, source0, 2, 26, 2)

    def restrict0(index, carry):
        pairs0[index] = residual_pair(second0, source0, 6 + 2 * index)[8:40, 0:128]
        return carry

    lax.fori_loop(0, 8, restrict0, 0)

    coarse = selected(row_pairs(pairs0, 8, 16), halving(64)).reshape(8, 16, 128)
    lane16 = lane_of((16, 128))
    for x in range(4):
        slabs1[1, x, 8:24, :] = jnp.where(lane16 < 64, coarse[x], coarse[x + 4])
    edge = ((lane16 >= 64) & (lane16 < 72)) | (lane16 >= 120)
    total = jnp.zeros((16, 128), F32)
    for x in range(8):
        total = total + turned(jnp.where(edge, coarse[x], 0.0), 16 * x + 8, 1)
    packed1[...] = total
    rows_from = {-1: (8, 8), 0: (0, 16), 1: (0, 8)}
    rows_to = {-1: 0, 0: 8, 1: 24}
    round_c = []
    for index, (dx, dy, dz) in enumerate(NEAR):
        (row, rows), peer = rows_from[dy], (-dx, -dy, -dz)
        if dz == 0:
            origin = slabs1.at[1, :, pl.ds(8 + row, rows), :]
            target = slabs1.at[dx + 1, :, pl.ds(rows_to[dy], rows), :]
        else:
            origin = packed1.at[pl.ds(row, rows), :]
            target = sides1.at[(dz + 1) // 2, dx + 1, pl.ds(rows_to[dy], rows), :]
        round_c.append(remote(origin, target, send_c, recv_c, index, peer))
    launch(round_c)
    arrive(round_c)
    for group in range(3):
        joined = jnp.where((lane32 // 8) % 2 == 0, sides1[0, group], sides1[1, group])
        for x in range(8):
            main = slabs1[group, x % 4]
            if x >= 4:
                main = turned(main, 64, 1)
            side = turned(joined, -(16 * x + 8), 1)
            source1[group * 8 + x] = jnp.where(lane32 < 64, main, side)
    sweep(first1, source1, source1, 1, 23, 2)
    sweep(second1, first1, source1, 2, 22, 4)
    for index in range(4):
        pairs1[index] = residual_pair(second1, source1, 8 + 2 * index)[8:24, :]

    coarse = selected(row_pairs(pairs1, 4, 8), halving(32)).reshape(4, 8, 128)
    group8 = lane_of((8, 128)) // 32
    for step in (-1, 0, 1):
        total = coarse[3]
        for x in range(3):
            total = jnp.where(group8 == (x + step) % 4, coarse[x], total)
        if step == 0:
            blocks2[1, 2, 8:16, :] = total
        else:
            packed2[(step + 1) // 2] = total
    round_d = []
    for index, (dx, dy, dz) in enumerate(WIDE):
        origin = blocks2.at[1, 2, pl.ds(8, 8), :] if dz == 0 else packed2.at[(dz + 1) // 2]
        target = blocks2.at[dz + 1, dx + 2, pl.ds(8 * dy + 8, 8), :]
        round_d.append(remote(origin, target, send_d, recv_d, index, (-dx, -dy, -dz)))
    launch(round_d)
    arrive(round_d)
    group24 = lane_of((24, 128)) // 32
    for block in range(5):
        for x in range(4):
            value = jnp.where(group24 == (x + 1) % 4, blocks2[2, block], blocks2[0, block])
            value = jnp.where(group24 == x, blocks2[1, block], value)
            source2[block * 4 + x] = turned(value, -32 * x, 1)
    sweep(first2, source2, source2, 1, 19, 6)
    sweep(second2, first2, source2, 2, 18, 4)
    for index in range(2):
        pairs2[index] = residual_pair(second2, source2, 8 + 2 * index)[8:16, :]

    lines3[0] = selected(row_pairs(pairs2, 2, 4), halving(16))
    round_e = [
        remote(lines3.at[0], lines3.at[z], send_e, recv_e, z - 1, (0, 0, -z)) for z in range(1, COUNT_Z)
    ]
    launch(round_e)
    arrive(round_e)
    group8 = lane_of((8, 128)) // 16
    line = lines3[0]
    for z in range(1, COUNT_Z):
        line = jnp.where(group8 == z, lines3[z], line)
    gathered3[0, 0] = line
    round_f = [
        remote(gathered3.at[0, 0], gathered3.at[a, b], send_f, recv_f, index, (-a, -b, 0))
        for index, (a, b) in enumerate(PLANE)
    ]
    launch(round_f)
    arrive(round_f)
    for a in range(COUNT_X):
        for b in range(COUNT_Y):
            for x in range(2):
                source3[2 * a + x, 4 * b : 4 * b + 4, :] = gathered3[a, b, 4 * x : 4 * x + 4, :]

    def mixed_whole(value):
        below = jnp.concatenate([value[-1:], value[:-1]], axis=0)
        above = jnp.concatenate([value[1:], value[:1]], axis=0)
        return mixed(value, below, above)

    right = source3[...]
    value = right
    for repeat in range(SWEEPS - 1):
        value = mixed_whole(value) + right
    rest = mixed_whole(value) + right - value
    level3[...] = value
    rest = rest.reshape(8, 2, 16, 128)
    pairs3[...] = rest[:, 0] + rest[:, 1]

    coarse = selected(row_pairs(pairs3, 8, 8), halving(64)).reshape(8, 8, 128)
    error = lax.fori_loop(
        0, COARSE_ITERS - 1, lambda index, current: mixed_whole(current) + coarse, coarse
    )

    straight, wrapped = doubling(256, False), doubling(128, True)
    spread = selected(error.reshape(64, 128), straight[:, 0:128]).reshape(8, 8, 128)
    for x in range(8):
        pairs3[x, pl.ds(0, 8, stride=2), :] = spread[x]
        pairs3[x, pl.ds(1, 8, stride=2), :] = spread[x]
    spread = jnp.broadcast_to(pairs3[...][:, None], (8, 2, 16, 128)).reshape(16, 16, 128)
    value = level3[...] + spread
    for repeat in range(SWEEPS):
        value = mixed_whole(value) + right

    near = jnp.concatenate([value[13:16], value[0:5]], axis=0)
    near = turned(near, 4, 1)
    spread = selected(near.reshape(128, 128), wrapped).reshape(8, 16, 128)
    for x in range(8):
        spread2[x, pl.ds(0, 12, stride=2), :] = spread[x, 0:12]
        spread2[x, pl.ds(1, 12, stride=2), :] = spread[x, 0:12]
    for x in range(8):
        for side in range(2):
            second2[2 + 2 * x + side] = second2[2 + 2 * x + side] + spread2[x]
    sweep(first2, second2, source2, 3, 17, 7)
    sweep(second2, first2, source2, 4, 16, 6)
    sweep(first2, second2, source2, 5, 15, 5)

    near = first2[5:15, 4:20, :]
    spread = selected(near.reshape(160, 128), wrapped).reshape(10, 16, 128)
    for x in range(10):
        spread1[x, pl.ds(0, 16, stride=2), :] = spread[x]
        spread1[x, pl.ds(1, 16, stride=2), :] = spread[x]
    for x in range(10):
        for side in range(2):
            second1[2 + 2 * x + side] = second1[2 + 2 * x + side] + spread1[x]
    sweep(first1, second1, source1, 3, 21, 3)
    sweep(second1, first1, source1, 4, 20, 4)
    sweep(first1, second1, source1, 5, 19, 2)

    near = first1[6:18, 4:28, :]
    spread = selected(near.reshape(288, 128), straight).reshape(12, 24, 256)
    for x in range(12):
        for half in range(2):
            lanes = slice(half * 128, half * 128 + 128)
            spread0[half, x, pl.ds(0, 24, stride=2), :] = spread[x, :, lanes]
            spread0[half, x, pl.ds(1, 24, stride=2), :] = spread[x, :, lanes]

    def correct0(index, carry):
        for half in range(2):
            lanes = slice(half * 128, half * 128 + 128)
            for side in range(2):
                x = 2 + 2 * index + side
                second0[x, :, lanes] = second0[x, :, lanes] + spread0[half, index]
        return carry

    lax.fori_loop(0, 12, correct0, 0)
    sweep(first0, second0, source0, 3, 25, 2)
    sweep(second0, first0, source0, 4, 24, 2)
    sweep(first0, second0, source0, 5, 23, 2)

    def finish(x, carry):
        whole = first0[6 + x]
        here = whole[8:40, 0:128]
        above_x = first0[7 + x, 8:40, 0:128]
        above_y = turned(whole[:, 0:128], -1, 0)[8:40]
        above_z = turned(whole[8:40], -1, 1)[:, 0:128]
        rows = pl.ds(pl.multiple_of(x * 32, 32), 32)
        result[0, rows, :] = field[0, rows, :] - (above_x - here)
        result[1, rows, :] = field[1, rows, :] - (above_y - here)
        result[2, rows, :] = field[2, rows, :] - (above_z - here)
        return carry

    lax.fori_loop(0, 16, finish, 0)
    stores = [pltpu.make_async_copy(result.at[c], cleaned.at[c], store_sem.at[c]) for c in range(3)]
    for store in stores:
        store.start()
    for copy in pending:
        copy.wait_send()
    for store in stores:
        store.wait()


def scratch_shapes():
    def vmem(*shape):
        return pltpu.VMEM(shape, F32)

    dma = pltpu.SemaphoreType.DMA
    return [
        vmem(3, 512, 128), vmem(3, 512, 128), vmem(32, 128), vmem(16, 128), vmem(32, 128), vmem(16, 128), vmem(32, 128),
        vmem(28, 48, 256), vmem(28, 48, 256), vmem(28, 48, 256), vmem(32, 256), vmem(2, 48, 512), vmem(8, 32, 128), vmem(2, 12, 48, 128),
        vmem(3, 4, 32, 128), vmem(16, 128), vmem(2, 3, 32, 128), vmem(24, 32, 128), vmem(24, 32, 128), vmem(24, 32, 128), vmem(4, 16, 128), vmem(10, 32, 128),
        vmem(2, 8, 128), vmem(3, 5, 24, 128), vmem(20, 24, 128), vmem(20, 24, 128), vmem(20, 24, 128), vmem(2, 8, 128), vmem(8, 24, 128),
        vmem(8, 8, 128), vmem(8, 4, 8, 128), vmem(16, 16, 128), vmem(16, 16, 128), vmem(8, 16, 128),
        dma((3,)), dma((3,)),
        dma((3,)), dma((3,)), dma((26,)), dma((26,)), dma((26,)), dma((26,)), dma((44,)), dma((44,)), dma((7,)), dma((7,)), dma((31,)), dma((31,)),
    ]


def body(magnetic):
    cleaned = pl.pallas_call(
        kernel,
        out_shape=jax.ShapeDtypeStruct((3, 512, 128), F32),
        in_specs=[pl.BlockSpec(memory_space=pl.ANY)],
        out_specs=pl.BlockSpec(memory_space=pl.ANY),
        scratch_shapes=scratch_shapes(),
        compiler_params=pltpu.CompilerParams(
            collective_id=0, has_side_effects=True, vmem_limit_bytes=32 << 20
        ),
    )(magnetic.reshape(3, 512, 128))
    return cleaned.reshape(3, 16, 32, 128)


def solution(mesh):
    spec = P(None, "gx", "gy", "gz")
    return jax.shard_map(body, mesh=mesh, in_specs=(spec,), out_specs=spec, check_vma=False)
```

time: 575 us -> 63.7 us (0.11); the launches traced: 567 us -> 63.6 us
  starting transfers between devices: 229 us -> 0 us
  waiting for transfers between devices: 203 us -> 0 us
  blocking collectives: 63.2 us -> 0 us
  Pallas kernels: 0 us -> 61.6 us
  local copies, waits for them, and re-layouts: 51.6 us -> 2.01 us
  other arithmetic: 17.5 us -> 0 us
    ppermute x152 -> x0, starting transfers between devices: 229 us -> none  [the longest x75 147 us: extended(): lax.ppermute(lax.slice_in_dim(block, 0, width, axis=dim), axis, backward)]
    ppermute x152 -> x0, waiting for transfers between devices: 203 us -> none  [the longest x75 119 us: extended(): lax.ppermute(lax.slice_in_dim(block, 0, width, axis=dim), axis, backward)]
    all_gather x1 -> x0, blocking collectives: 63.2 us -> none  [collect(): lax.all_gather(source[None], ('gx', 'gy', 'gz'), axis=0, tiled=True)]
    pallas_call x0 -> x1, Pallas kernels: none -> 61.6 us  [body(): pl.pallas_call(kernel, out_shape=jax.ShapeDtypeStruct((3, 512, 128), F32)...]
    reshape x7 -> x0, local copies, waits for them, and re-layouts: 35 us -> none  [the longest x3 20.4 us: restrict(): values.reshape(extent[0] // 2, 2, extent[1] // 2, 2, extent[2] // 2, 2)]
    slice x191 -> x0, local copies, waits for them, and re-layouts: 8.34 us -> none  [the longest x46 3.39 us: apply_local(): beside = beside + jnp.roll(values, -1, 2) + jnp.roll(values, 1, 2)]
    reduce_sum x5 -> x0, other arithmetic: 7.51 us -> none  [restrict(): return jnp.sum(blocks, axis=(1, 3, 5)) * 0.125]
    broadcast_in_dim x6 -> x0, local copies, waits for them, and re-layouts: 7.1 us -> none  [prolong(): jnp.broadcast_to(values[:, None, :, None, :, None], (extent[0], 2, extent...]
  transfers between devices with their start and end apart: 152 -> 0, of which waited for: 149 -> 0; matrix products, arithmetic and copies ran while one was open for 0% -> 0% of each run, Pallas kernels for 0% -> 0%
where the time goes in v1:
time: 63.7 us; the launch traced here: 63.6 us
  Pallas kernels  61.6 us (97%)
  local copies, waits for them, and re-layouts  2.01 us (3%)
    pallas_call x1, Pallas kernels, body(): pl.pallas_call(kernel, out_shape=jax.ShapeDtypeStruct((3, 512, 128), F32)...  61.6 us
    unnamed x3, local copies, waits for them, and re-layouts  2.01 us

profile of v1, /device:TPU:1, one launch (start us, length us, event | category | flops | bytes accessed | tf_op | source)
XLA Modules:
  0.0 63.6 jit_solution(4832272032247195126)
XLA Ops:
  0.0 0.0 copy-start
  0.0 1.1 %copy-done = f32[3,16,32,128]{3,2,1,0:T(8,128)S(1)} copy-done((f32[3,16,32,128]{3,2,1,0:T(8,128)S(1)}, f32[3,16,32,128]{3,2,1,0:T(8,128)}, u32[]{:S(2)}) %copy-start) | copy-done | bytes 786456
  1.1 61.6 %shard_map.17 = f32[3,512,128]{2,1,0:T(8,128)S(1)} custom-call(f32[3,512,128]{2,1,0:T(8,128)S(1)} %bitcast.3), custom_call_target="tpu_custom_call" | custom-call | tf_op jit(solution)/shard_map/pallas_call | solution.py:408
  62.7 0.9 %copy.3 = f32[3,16,32,128]{3,2,1,0:T(8,128)} copy(f32[3,16,32,128]{3,2,1,0:T(8,128)S(1)} %bitcast.2) | data formatting | bytes 1572864
Async XLA Ops:
  0.0 1.1 %copy-start = (f32[3,16,32,128]{3,2,1,0:T(8,128)S(1)}, f32[3,16,32,128]{3,2,1,0:T(8,128)}, u32[]{:S(2)}) copy-start(f32[3,16,32,128]{3,2,1,0:T(8,128)} %param.1) | copy-start | bytes 2359300

commit v2 on v1

--- a/solution.py
+++ b/solution.py
@@ -1,4 +1,3 @@
-import functools
 import itertools
 
 import jax
@@ -12,10 +11,18 @@
 COARSE_ITERS = 24
 MESH = pl.DeviceIdType.MESH
 F32 = jnp.float32
-NEAR = [d for d in itertools.product((-1, 0, 1), repeat=3) if d != (0, 0, 0)]
-WIDE = NEAR + [(dx, dy, dz) for dx in (-2, 2) for dy in (-1, 0, 1) for dz in (-1, 0, 1)]
 COUNT_X, COUNT_Y, COUNT_Z = 8, 4, 8
-PLANE = [(a, b) for a in range(COUNT_X) for b in range(COUNT_Y) if (a, b) != (0, 0)]
+NEAR = sorted(
+    (d for d in itertools.product((-1, 0, 1), repeat=3) if d != (0, 0, 0)),
+    key=lambda d: -sum(map(abs, d)),
+)
+BULKY = sorted(NEAR, key=lambda d: d not in [(0, 1, 0), (0, -1, 0), (1, 0, 0), (-1, 0, 0)])
+WIDE = [(dx, dy, dz) for dx in (-2, 2) for dy in (-1, 0, 1) for dz in (-1, 0, 1)]
+LINE = sorted(range(1, COUNT_Z), key=lambda z: -min(z, COUNT_Z - z))
+PLANE = sorted(
+    ((a, b) for a in range(COUNT_X) for b in range(COUNT_Y) if (a, b) != (0, 0)),
+    key=lambda d: -min(d[0], COUNT_X - d[0]) - 2 * min(d[1], COUNT_Y - d[1]),
+)
 SEVENTH = 1.0 / 7.0
 
 
@@ -49,7 +56,7 @@
         target[pl.ds(at, step)] = mean + source[pl.ds(at, step)]
         return carry
 
-    lax.fori_loop(0, (high - low) // step, body, 0)
+    lax.fori_loop(0, (high - low) // step, body, 0, unroll=True)
 
 
 def residual_pair(current, source, at):
@@ -60,11 +67,13 @@
 
 
 def selected(value, matrix):
-    high = value.astype(jnp.bfloat16)
-    low = (value - high.astype(F32)).astype(jnp.bfloat16)
-    return jnp.dot(high, matrix, preferred_element_type=F32) + jnp.dot(
-        low, matrix, preferred_element_type=F32
-    )
+    total = None
+    for term in range(3):
+        part = value.astype(jnp.bfloat16)
+        value = value - part.astype(F32)
+        product = jnp.dot(part, matrix, preferred_element_type=F32)
+        total = product if total is None else total + product
+    return total
 
 
 def halving(period):
@@ -88,14 +97,14 @@
     return jnp.concatenate(pieces, axis=0)
 
 
-def kernel(magnetic, cleaned, *scratch):
+def kernel(field, result, *scratch):
     (
-        field, result, low_x, low_y, low_z, last_y, last_z,
+        low_x, low_y, low_z, last_y, last_z,
         source0, first0, second0, packed0, sides0, pairs0, spread0,
         slabs1, packed1, sides1, source1, first1, second1, pairs1, spread1,
         packed2, blocks2, source2, first2, second2, pairs2, spread2,
         lines3, gathered3, source3, level3, pairs3,
-        load_sem, store_sem,
+        halve0, halve1, halve2, straight, wrapped,
         send_a, recv_a, send_b, recv_b, send_c, recv_c, send_d, recv_d, send_e, recv_e, send_f, recv_f,
     ) = scratch
     me = (lax.axis_index("gx"), lax.axis_index("gy"), lax.axis_index("gz"))
@@ -110,25 +119,21 @@
             device_id=at(offset), device_id_type=MESH,
         )
 
-    pending = []
-
     def launch(copies):
         for copy in copies:
             copy.start()
-        pending.extend(copies)
+
+    def sent(copies):
+        for copy in copies:
+            copy.wait_send()
 
     def arrive(copies):
         for copy in copies:
             copy.wait_recv()
 
-    loads = [pltpu.make_async_copy(magnetic.at[c], field.at[c], load_sem.at[c]) for c in range(3)]
-    for load in loads:
-        load.start()
     barrier = pltpu.get_barrier_semaphore()
     for offset in NEAR:
         pl.semaphore_signal(barrier, inc=1, device_id=at(offset), device_id_type=MESH)
-    for load in loads:
-        load.wait()
 
     lane32 = lane_of((32, 128))
     row32 = row_of((32, 128))
@@ -174,7 +179,7 @@
     lanes_from = {-1: (128, 128), 0: (0, 256), 1: (0, 128)}
     lanes_to = {-1: 0, 0: 128, 1: 384}
     round_b = []
-    for index, (dx, dy, dz) in enumerate(NEAR):
+    for index, (dx, dy, dz) in enumerate(BULKY):
         (row, rows), peer = rows_from[dy], (-dx, -dy, -dz)
         if dz == 0:
             plane, planes = planes_from[dx]
@@ -186,6 +191,12 @@
             target = sides0.at[(dz + 1) // 2, pl.ds(rows_to[dy], rows), pl.ds(lanes_to[dx], lanes)]
         round_b.append(remote(origin, target, send_b, recv_b, index, peer))
     launch(round_b)
+    sent(round_a)
+    halve0[...] = halving(64)
+    halve1[...] = halving(32)
+    halve2[...] = halving(16)
+    straight[...] = doubling(256, False)
+    wrapped[...] = doubling(128, True)
     arrive(round_b)
 
     lane48 = lane_of((48, 128))
@@ -196,16 +207,16 @@
             x = group * 8 + slot - 8
             if -6 <= x < 22:
                 source0[6 + x, :, 128:256] = turned(joined, -16 * slot, 1)
-    sweep(first0, source0, source0, 1, 27, 2)
-    sweep(second0, first0, source0, 2, 26, 2)
+    sweep(first0, source0, source0, 4, 24, 2)
+    sweep(second0, first0, source0, 5, 23, 2)
 
     def restrict0(index, carry):
         pairs0[index] = residual_pair(second0, source0, 6 + 2 * index)[8:40, 0:128]
         return carry
 
-    lax.fori_loop(0, 8, restrict0, 0)
-
-    coarse = selected(row_pairs(pairs0, 8, 16), halving(64)).reshape(8, 16, 128)
+    lax.fori_loop(0, 8, restrict0, 0, unroll=True)
+
+    coarse = selected(row_pairs(pairs0, 8, 16), halve0[...]).reshape(8, 16, 128)
     lane16 = lane_of((16, 128))
     for x in range(4):
         slabs1[1, x, 8:24, :] = jnp.where(lane16 < 64, coarse[x], coarse[x + 4])
@@ -227,6 +238,11 @@
             target = sides1.at[(dz + 1) // 2, dx + 1, pl.ds(rows_to[dy], rows), :]
         round_c.append(remote(origin, target, send_c, recv_c, index, peer))
     launch(round_c)
+    sent(round_b)
+    sweep(first0, source0, source0, 1, 4, 3)
+    sweep(first0, source0, source0, 24, 27, 3)
+    sweep(second0, first0, source0, 2, 5, 3)
+    sweep(second0, first0, source0, 23, 26, 3)
     arrive(round_c)
     for group in range(3):
         joined = jnp.where((lane32 // 8) % 2 == 0, sides1[0, group], sides1[1, group])
@@ -236,12 +252,12 @@
                 main = turned(main, 64, 1)
             side = turned(joined, -(16 * x + 8), 1)
             source1[group * 8 + x] = jnp.where(lane32 < 64, main, side)
-    sweep(first1, source1, source1, 1, 23, 2)
-    sweep(second1, first1, source1, 2, 22, 4)
+    sweep(first1, source1, source1, 6, 18, 4)
+    sweep(second1, first1, source1, 7, 17, 5)
     for index in range(4):
         pairs1[index] = residual_pair(second1, source1, 8 + 2 * index)[8:24, :]
 
-    coarse = selected(row_pairs(pairs1, 4, 8), halving(32)).reshape(4, 8, 128)
+    coarse = selected(row_pairs(pairs1, 4, 8), halve1[...]).reshape(4, 8, 128)
     group8 = lane_of((8, 128)) // 32
     for step in (-1, 0, 1):
         total = coarse[3]
@@ -252,28 +268,45 @@
         else:
             packed2[(step + 1) // 2] = total
     round_d = []
-    for index, (dx, dy, dz) in enumerate(WIDE):
+    for index, (dx, dy, dz) in enumerate(NEAR + WIDE):
         origin = blocks2.at[1, 2, pl.ds(8, 8), :] if dz == 0 else packed2.at[(dz + 1) // 2]
         target = blocks2.at[dz + 1, dx + 2, pl.ds(8 * dy + 8, 8), :]
         round_d.append(remote(origin, target, send_d, recv_d, index, (-dx, -dy, -dz)))
     launch(round_d)
-    arrive(round_d)
+    sent(round_c)
+    sweep(first1, source1, source1, 1, 6, 5)
+    sweep(first1, source1, source1, 18, 23, 5)
+    sweep(second1, first1, source1, 2, 7, 5)
+    sweep(second1, first1, source1, 17, 22, 5)
+    arrive(round_d[: len(NEAR)])
     group24 = lane_of((24, 128)) // 32
-    for block in range(5):
+
+    def unpack2(block):
         for x in range(4):
             value = jnp.where(group24 == (x + 1) % 4, blocks2[2, block], blocks2[0, block])
             value = jnp.where(group24 == x, blocks2[1, block], value)
             source2[block * 4 + x] = turned(value, -32 * x, 1)
-    sweep(first2, source2, source2, 1, 19, 6)
-    sweep(second2, first2, source2, 2, 18, 4)
+
+    for block in (1, 2, 3):
+        unpack2(block)
+    sweep(first2, source2, source2, 6, 14, 4)
+    sweep(second2, first2, source2, 7, 13, 6)
     for index in range(2):
         pairs2[index] = residual_pair(second2, source2, 8 + 2 * index)[8:16, :]
 
-    lines3[0] = selected(row_pairs(pairs2, 2, 4), halving(16))
+    lines3[0] = selected(row_pairs(pairs2, 2, 4), halve2[...])
     round_e = [
-        remote(lines3.at[0], lines3.at[z], send_e, recv_e, z - 1, (0, 0, -z)) for z in range(1, COUNT_Z)
+        remote(lines3.at[0], lines3.at[z], send_e, recv_e, z - 1, (0, 0, -z)) for z in LINE
     ]
     launch(round_e)
+    sent(round_d)
+    arrive(round_d[len(NEAR) :])
+    unpack2(0)
+    unpack2(4)
+    sweep(first2, source2, source2, 1, 6, 5)
+    sweep(first2, source2, source2, 14, 19, 5)
+    sweep(second2, first2, source2, 2, 7, 5)
+    sweep(second2, first2, source2, 13, 18, 5)
     arrive(round_e)
     group8 = lane_of((8, 128)) // 16
     line = lines3[0]
@@ -285,6 +318,7 @@
         for index, (a, b) in enumerate(PLANE)
     ]
     launch(round_f)
+    sent(round_e)
     arrive(round_f)
     for a in range(COUNT_X):
         for b in range(COUNT_Y):
@@ -305,12 +339,11 @@
     rest = rest.reshape(8, 2, 16, 128)
     pairs3[...] = rest[:, 0] + rest[:, 1]
 
-    coarse = selected(row_pairs(pairs3, 8, 8), halving(64)).reshape(8, 8, 128)
+    coarse = selected(row_pairs(pairs3, 8, 8), halve0[...]).reshape(8, 8, 128)
     error = lax.fori_loop(
         0, COARSE_ITERS - 1, lambda index, current: mixed_whole(current) + coarse, coarse
     )
 
-    straight, wrapped = doubling(256, False), doubling(128, True)
     spread = selected(error.reshape(64, 128), straight[:, 0:128]).reshape(8, 8, 128)
     for x in range(8):
         pairs3[x, pl.ds(0, 8, stride=2), :] = spread[x]
@@ -322,7 +355,7 @@
 
     near = jnp.concatenate([value[13:16], value[0:5]], axis=0)
     near = turned(near, 4, 1)
-    spread = selected(near.reshape(128, 128), wrapped).reshape(8, 16, 128)
+    spread = selected(near.reshape(128, 128), wrapped[...]).reshape(8, 16, 128)
     for x in range(8):
         spread2[x, pl.ds(0, 12, stride=2), :] = spread[x, 0:12]
         spread2[x, pl.ds(1, 12, stride=2), :] = spread[x, 0:12]
@@ -334,7 +367,7 @@
     sweep(first2, second2, source2, 5, 15, 5)
 
     near = first2[5:15, 4:20, :]
-    spread = selected(near.reshape(160, 128), wrapped).reshape(10, 16, 128)
+    spread = selected(near.reshape(160, 128), wrapped[...]).reshape(10, 16, 128)
     for x in range(10):
         spread1[x, pl.ds(0, 16, stride=2), :] = spread[x]
         spread1[x, pl.ds(1, 16, stride=2), :] = spread[x]
@@ -346,7 +379,7 @@
     sweep(first1, second1, source1, 5, 19, 2)
 
     near = first1[6:18, 4:28, :]
-    spread = selected(near.reshape(288, 128), straight).reshape(12, 24, 256)
+    spread = selected(near.reshape(288, 128), straight[...]).reshape(12, 24, 256)
     for x in range(12):
         for half in range(2):
             lanes = slice(half * 128, half * 128 + 128)
@@ -361,7 +394,7 @@
                 second0[x, :, lanes] = second0[x, :, lanes] + spread0[half, index]
         return carry
 
-    lax.fori_loop(0, 12, correct0, 0)
+    lax.fori_loop(0, 12, correct0, 0, unroll=True)
     sweep(first0, second0, source0, 3, 25, 2)
     sweep(second0, first0, source0, 4, 24, 2)
     sweep(first0, second0, source0, 5, 23, 2)
@@ -378,28 +411,25 @@
         result[2, rows, :] = field[2, rows, :] - (above_z - here)
         return carry
 
-    lax.fori_loop(0, 16, finish, 0)
-    stores = [pltpu.make_async_copy(result.at[c], cleaned.at[c], store_sem.at[c]) for c in range(3)]
-    for store in stores:
-        store.start()
-    for copy in pending:
-        copy.wait_send()
-    for store in stores:
-        store.wait()
+    lax.fori_loop(0, 16, finish, 0, unroll=True)
+    sent(round_f)
 
 
 def scratch_shapes():
     def vmem(*shape):
         return pltpu.VMEM(shape, F32)
 
+    def half(lanes):
+        return pltpu.VMEM((128, lanes), jnp.bfloat16)
+
     dma = pltpu.SemaphoreType.DMA
     return [
-        vmem(3, 512, 128), vmem(3, 512, 128), vmem(32, 128), vmem(16, 128), vmem(32, 128), vmem(16, 128), vmem(32, 128),
+        vmem(32, 128), vmem(16, 128), vmem(32, 128), vmem(16, 128), vmem(32, 128),
         vmem(28, 48, 256), vmem(28, 48, 256), vmem(28, 48, 256), vmem(32, 256), vmem(2, 48, 512), vmem(8, 32, 128), vmem(2, 12, 48, 128),
         vmem(3, 4, 32, 128), vmem(16, 128), vmem(2, 3, 32, 128), vmem(24, 32, 128), vmem(24, 32, 128), vmem(24, 32, 128), vmem(4, 16, 128), vmem(10, 32, 128),
         vmem(2, 8, 128), vmem(3, 5, 24, 128), vmem(20, 24, 128), vmem(20, 24, 128), vmem(20, 24, 128), vmem(2, 8, 128), vmem(8, 24, 128),
         vmem(8, 8, 128), vmem(8, 4, 8, 128), vmem(16, 16, 128), vmem(16, 16, 128), vmem(8, 16, 128),
-        dma((3,)), dma((3,)),
+        half(128), half(128), half(128), half(256), half(128),
         dma((3,)), dma((3,)), dma((26,)), dma((26,)), dma((26,)), dma((26,)), dma((44,)), dma((44,)), dma((7,)), dma((7,)), dma((31,)), dma((31,)),
     ]
 
@@ -408,8 +438,8 @@
     cleaned = pl.pallas_call(
         kernel,
         out_shape=jax.ShapeDtypeStruct((3, 512, 128), F32),
-        in_specs=[pl.BlockSpec(memory_space=pl.ANY)],
-        out_specs=pl.BlockSpec(memory_space=pl.ANY),
+        in_specs=[pl.BlockSpec(memory_space=pltpu.VMEM)],
+        out_specs=pl.BlockSpec(memory_space=pltpu.VMEM),
         scratch_shapes=scratch_shapes(),
         compiler_params=pltpu.CompilerParams(
             collective_id=0, has_side_effects=True, vmem_limit_bytes=32 << 20

time: 63.7 us -> 51.3 us (0.81)
  Pallas kernels: 61.6 us -> 49.2 us
    pallas_call x1, Pallas kernels: 61.6 us -> 49.2 us  [body(): pl.pallas_call(kernel, out_shape=jax.ShapeDtypeStruct((3, 512, 128), F32)...]
where the time goes in v2:
time: 51.3 us; the launch traced here: 51.2 us
  Pallas kernels  49.2 us (96%)
  local copies, waits for them, and re-layouts  2.01 us (4%)
    pallas_call x1, Pallas kernels, body(): pl.pallas_call(kernel, out_shape=jax.ShapeDtypeStruct((3, 512, 128), F32)...  49.2 us
    unnamed x3, local copies, waits for them, and re-layouts  2.01 us

profile of v2, /device:TPU:1, one launch (start us, length us, event | category | flops | bytes accessed | tf_op | source)
XLA Modules:
  0.0 51.2 jit_solution(14313618689565120208)
XLA Ops:
  0.0 0.0 copy-start
  0.0 1.1 %copy-done = f32[3,16,32,128]{3,2,1,0:T(8,128)S(1)} copy-done((f32[3,16,32,128]{3,2,1,0:T(8,128)S(1)}, f32[3,16,32,128]{3,2,1,0:T(8,128)}, u32[]{:S(2)}) %copy-start) | copy-done | bytes 786456
  1.1 49.2 %shard_map.17 = f32[3,512,128]{2,1,0:T(8,128)S(1)} custom-call(f32[3,512,128]{2,1,0:T(8,128)S(1)} %bitcast.3), custom_call_target="tpu_custom_call" | custom-call | tf_op jit(solution)/shard_map/pallas_call | solution.py:438
  50.3 0.9 %copy.3 = f32[3,16,32,128]{3,2,1,0:T(8,128)} copy(f32[3,16,32,128]{3,2,1,0:T(8,128)S(1)} %bitcast.2) | data formatting | bytes 1572864
Async XLA Ops:
  0.0 1.1 %copy-start = (f32[3,16,32,128]{3,2,1,0:T(8,128)S(1)}, f32[3,16,32,128]{3,2,1,0:T(8,128)}, u32[]{:S(2)}) copy-start(f32[3,16,32,128]{3,2,1,0:T(8,128)} %param.1) | copy-start | bytes 2359300

commit v3 on v2

--- a/solution.py
+++ b/solution.py
@@ -16,6 +16,7 @@
     (d for d in itertools.product((-1, 0, 1), repeat=3) if d != (0, 0, 0)),
     key=lambda d: -sum(map(abs, d)),
 )
+GREETED = [d for d in NEAR if sum(map(abs, d)) != 2]
 BULKY = sorted(NEAR, key=lambda d: d not in [(0, 1, 0), (0, -1, 0), (1, 0, 0), (-1, 0, 0)])
 WIDE = [(dx, dy, dz) for dx in (-2, 2) for dy in (-1, 0, 1) for dz in (-1, 0, 1)]
 LINE = sorted(range(1, COUNT_Z), key=lambda z: -min(z, COUNT_Z - z))
@@ -97,14 +98,15 @@
     return jnp.concatenate(pieces, axis=0)
 
 
-def kernel(field, result, *scratch):
+def kernel(magnetic, result, *scratch):
     (
-        low_x, low_y, low_z, last_y, last_z,
+        field, low_x, low_y, low_z, last_y, last_z,
         source0, first0, second0, packed0, sides0, pairs0, spread0,
         slabs1, packed1, sides1, source1, first1, second1, pairs1, spread1,
         packed2, blocks2, source2, first2, second2, pairs2, spread2,
         lines3, gathered3, source3, level3, pairs3,
         halve0, halve1, halve2, straight, wrapped,
+        load_sem, enter_sem,
         send_a, recv_a, send_b, recv_b, send_c, recv_c, send_d, recv_d, send_e, recv_e, send_f, recv_f,
     ) = scratch
     me = (lax.axis_index("gx"), lax.axis_index("gy"), lax.axis_index("gz"))
@@ -131,9 +133,14 @@
         for copy in copies:
             copy.wait_recv()
 
+    loads = [pltpu.make_async_copy(magnetic.at[c], field.at[c], load_sem.at[c]) for c in range(3)]
+    for load in loads:
+        load.start()
     barrier = pltpu.get_barrier_semaphore()
-    for offset in NEAR:
+    for offset in GREETED:
         pl.semaphore_signal(barrier, inc=1, device_id=at(offset), device_id_type=MESH)
+    for load in loads:
+        load.wait()
 
     lane32 = lane_of((32, 128))
     row32 = row_of((32, 128))
@@ -145,13 +152,16 @@
             lane32 == x, turned(field[2, x * 32 : x * 32 + 32, :], x + 1, 1), column
         )
     last_z[...] = column
-    pl.semaphore_wait(barrier, len(NEAR))
+    pl.semaphore_wait(barrier, len(GREETED))
     round_a = [
         remote(field.at[0, pl.ds(480, 32)], low_x, send_a, recv_a, 0, (1, 0, 0)),
         remote(last_y, low_y, send_a, recv_a, 1, (0, 1, 0)),
         remote(last_z, low_z, send_a, recv_a, 2, (0, 0, 1)),
     ]
     launch(round_a)
+    for offset in ((-1, 0, 0), (0, -1, 0), (0, 0, -1)):
+        pl.semaphore_signal(enter_sem, inc=1, device_id=at(offset), device_id_type=MESH)
+    pl.semaphore_wait(enter_sem, 3)
     arrive(round_a)
 
     column = low_z[...]
@@ -424,12 +434,13 @@
 
     dma = pltpu.SemaphoreType.DMA
     return [
-        vmem(32, 128), vmem(16, 128), vmem(32, 128), vmem(16, 128), vmem(32, 128),
+        vmem(3, 512, 128), vmem(32, 128), vmem(16, 128), vmem(32, 128), vmem(16, 128), vmem(32, 128),
         vmem(28, 48, 256), vmem(28, 48, 256), vmem(28, 48, 256), vmem(32, 256), vmem(2, 48, 512), vmem(8, 32, 128), vmem(2, 12, 48, 128),
         vmem(3, 4, 32, 128), vmem(16, 128), vmem(2, 3, 32, 128), vmem(24, 32, 128), vmem(24, 32, 128), vmem(24, 32, 128), vmem(4, 16, 128), vmem(10, 32, 128),
         vmem(2, 8, 128), vmem(3, 5, 24, 128), vmem(20, 24, 128), vmem(20, 24, 128), vmem(20, 24, 128), vmem(2, 8, 128), vmem(8, 24, 128),
         vmem(8, 8, 128), vmem(8, 4, 8, 128), vmem(16, 16, 128), vmem(16, 16, 128), vmem(8, 16, 128),
         half(128), half(128), half(128), half(256), half(128),
+        dma((3,)), pltpu.SemaphoreType.REGULAR,
         dma((3,)), dma((3,)), dma((26,)), dma((26,)), dma((26,)), dma((26,)), dma((44,)), dma((44,)), dma((7,)), dma((7,)), dma((31,)), dma((31,)),
     ]
 
@@ -438,11 +449,11 @@
     cleaned = pl.pallas_call(
         kernel,
         out_shape=jax.ShapeDtypeStruct((3, 512, 128), F32),
-        in_specs=[pl.BlockSpec(memory_space=pltpu.VMEM)],
+        in_specs=[pl.BlockSpec(memory_space=pl.ANY)],
         out_specs=pl.BlockSpec(memory_space=pltpu.VMEM),
         scratch_shapes=scratch_shapes(),
         compiler_params=pltpu.CompilerParams(
-            collective_id=0, has_side_effects=True, vmem_limit_bytes=32 << 20
+            collective_id=0, has_side_effects=True, vmem_limit_bytes=53 << 20
         ),
     )(magnetic.reshape(3, 512, 128))
     return cleaned.reshape(3, 16, 32, 128)

time: 51.3 us -> 50.1 us (0.977)
  local copies, waits for them, and re-layouts: 2.01 us -> 0.88 us
    unnamed x3 -> x1, local copies, waits for them, and re-layouts: 2.01 us -> 0.88 us
where the time goes in v3:
time: 50.1 us; the launch traced here: 50 us
  Pallas kernels  49.1 us (98%)
  local copies, waits for them, and re-layouts  0.88 us (2%)
    pallas_call x1, Pallas kernels, body(): pl.pallas_call(kernel, out_shape=jax.ShapeDtypeStruct((3, 512, 128), F32)...  49.1 us

profile of v3, /device:TPU:1, one launch (start us, length us, event | category | flops | bytes accessed | tf_op | source)
XLA Modules:
  0.0 50.0 jit_solution(4557427763304324991)
XLA Ops:
  0.0 49.1 %shard_map.17 = f32[3,512,128]{2,1,0:T(8,128)S(1)} custom-call(f32[3,512,128]{2,1,0:T(8,128)} %bitcast.3), custom_call_target="tpu_custom_call" | custom-call | tf_op jit(solution)/shard_map/pallas_call | solution.py:449
  49.1 0.9 %copy.3 = f32[3,16,32,128]{3,2,1,0:T(8,128)} copy(f32[3,16,32,128]{3,2,1,0:T(8,128)S(1)} %bitcast.2) | data formatting | bytes 1572864

commit v4 on v3

--- a/solution.py
+++ b/solution.py
@@ -351,7 +351,11 @@
 
     coarse = selected(row_pairs(pairs3, 8, 8), halve0[...]).reshape(8, 8, 128)
     error = lax.fori_loop(
-        0, COARSE_ITERS - 1, lambda index, current: mixed_whole(current) + coarse, coarse
+        0,
+        COARSE_ITERS - 1,
+        lambda index, current: mixed_whole(current) + coarse,
+        coarse,
+        unroll=True,
     )
 
     spread = selected(error.reshape(64, 128), straight[:, 0:128]).reshape(8, 8, 128)
@@ -360,10 +364,13 @@
         pairs3[x, pl.ds(1, 8, stride=2), :] = spread[x]
     spread = jnp.broadcast_to(pairs3[...][:, None], (8, 2, 16, 128)).reshape(16, 16, 128)
     value = level3[...] + spread
+    value = jnp.concatenate([value[10:16], value[0:8]], axis=0)
+    right = jnp.concatenate([right[10:16], right[0:8]], axis=0)
     for repeat in range(SWEEPS):
-        value = mixed_whole(value) + right
-
-    near = jnp.concatenate([value[13:16], value[0:5]], axis=0)
+        right = right[1:-1]
+        value = mixed(value[1:-1], value[:-2], value[2:]) + right
+
+    near = value
     near = turned(near, 4, 1)
     spread = selected(near.reshape(128, 128), wrapped[...]).reshape(8, 16, 128)
     for x in range(8):

time: 50.1 us -> 49.6 us (0.990)
  no operation moved by 1% of the time
where the time goes in v4:
time: 49.6 us; the launch traced here: 49.5 us
  Pallas kernels  48.6 us (98%)
  local copies, waits for them, and re-layouts  0.88 us (2%)
    pallas_call x1, Pallas kernels, body(): pl.pallas_call(kernel, out_shape=jax.ShapeDtypeStruct((3, 512, 128), F32)...  48.6 us

profile of v4, /device:TPU:1, one launch (start us, length us, event | category | flops | bytes accessed | tf_op | source)
XLA Modules:
  0.0 49.5 jit_solution(12837219208169562725)
XLA Ops:
  0.0 48.6 %shard_map.17 = f32[3,512,128]{2,1,0:T(8,128)S(1)} custom-call(f32[3,512,128]{2,1,0:T(8,128)} %bitcast.3), custom_call_target="tpu_custom_call" | custom-call | tf_op jit(solution)/shard_map/pallas_call | solution.py:456
  48.6 0.9 %copy.3 = f32[3,16,32,128]{3,2,1,0:T(8,128)} copy(f32[3,16,32,128]{3,2,1,0:T(8,128)S(1)} %bitcast.2) | data formatting | bytes 1572864

commit v5 on v4

--- a/solution.py
+++ b/solution.py
@@ -16,7 +16,7 @@
     (d for d in itertools.product((-1, 0, 1), repeat=3) if d != (0, 0, 0)),
     key=lambda d: -sum(map(abs, d)),
 )
-GREETED = [d for d in NEAR if sum(map(abs, d)) != 2]
+GREETED = [d for d in reversed(NEAR) if sum(map(abs, d)) != 2]
 BULKY = sorted(NEAR, key=lambda d: d not in [(0, 1, 0), (0, -1, 0), (1, 0, 0), (-1, 0, 0)])
 WIDE = [(dx, dy, dz) for dx in (-2, 2) for dy in (-1, 0, 1) for dz in (-1, 0, 1)]
 LINE = sorted(range(1, COUNT_Z), key=lambda z: -min(z, COUNT_Z - z))
@@ -184,8 +184,8 @@
 
     rows_from = {-1: (24, 8), 0: (0, 32), 1: (0, 8)}
     rows_to = {-1: 0, 0: 8, 1: 40}
-    planes_from = {-1: (10, 6), 0: (0, 16), 1: (0, 6)}
-    planes_to = {-1: 0, 0: 6, 1: 22}
+    planes_from = {-1: (11, 5), 0: (0, 16), 1: (0, 6)}
+    planes_to = {-1: 1, 0: 6, 1: 22}
     lanes_from = {-1: (128, 128), 0: (0, 256), 1: (0, 128)}
     lanes_to = {-1: 0, 0: 128, 1: 384}
     round_b = []
@@ -215,7 +215,7 @@
         joined = jnp.where((lane48 // 8) % 2 == 1, sides0[0, :, lanes], sides0[1, :, lanes])
         for slot in range(8):
             x = group * 8 + slot - 8
-            if -6 <= x < 22:
+            if -5 <= x < 22:
                 source0[6 + x, :, 128:256] = turned(joined, -16 * slot, 1)
     sweep(first0, source0, source0, 4, 24, 2)
     sweep(second0, first0, source0, 5, 23, 2)
@@ -249,9 +249,9 @@
         round_c.append(remote(origin, target, send_c, recv_c, index, peer))
     launch(round_c)
     sent(round_b)
-    sweep(first0, source0, source0, 1, 4, 3)
+    sweep(first0, source0, source0, 2, 4, 2)
     sweep(first0, source0, source0, 24, 27, 3)
-    sweep(second0, first0, source0, 2, 5, 3)
+    sweep(second0, first0, source0, 3, 5, 2)
     sweep(second0, first0, source0, 23, 26, 3)
     arrive(round_c)
     for group in range(3):
@@ -412,9 +412,9 @@
         return carry
 
     lax.fori_loop(0, 12, correct0, 0, unroll=True)
-    sweep(first0, second0, source0, 3, 25, 2)
-    sweep(second0, first0, source0, 4, 24, 2)
-    sweep(first0, second0, source0, 5, 23, 2)
+    sweep(first0, second0, source0, 4, 25, 3)
+    sweep(second0, first0, source0, 5, 24, 1)
+    sweep(first0, second0, source0, 6, 23, 1)
 
     def finish(x, carry):
         whole = first0[6 + x]

time: 49.6 us -> 49.7 us (level)
  no operation moved by 1% of the time
where the time goes in v5:
time: 49.7 us; the launch traced here: 49.6 us
  Pallas kernels  48.7 us (98%)
  local copies, waits for them, and re-layouts  0.88 us (2%)
    pallas_call x1, Pallas kernels, body(): pl.pallas_call(kernel, out_shape=jax.ShapeDtypeStruct((3, 512, 128), F32)...  48.7 us

profile of v5, /device:TPU:1, one launch (start us, length us, event | category | flops | bytes accessed | tf_op | source)
XLA Modules:
  0.0 49.6 jit_solution(5183834364915276335)
XLA Ops:
  0.0 48.7 %shard_map.17 = f32[3,512,128]{2,1,0:T(8,128)S(1)} custom-call(f32[3,512,128]{2,1,0:T(8,128)} %bitcast.3), custom_call_target="tpu_custom_call" | custom-call | tf_op jit(solution)/shard_map/pallas_call | solution.py:456
  48.7 0.9 %copy.3 = f32[3,16,32,128]{3,2,1,0:T(8,128)} copy(f32[3,16,32,128]{3,2,1,0:T(8,128)S(1)} %bitcast.2) | data formatting | bytes 1572864
